TPU v7x, 256 devices: a whole 4x4x8 slice. The times are simulated.
256 devices in a mesh: cls: 2 (over y_hi), dom: 16 (over y_lo, x, core), orient: 8 (over z).
Axes of the slice: x: 4, y: 4 (y_hi: 2, y_lo: 2; y = y_hi * 2 + y_lo), z: 8, core: 2. Of those that a mesh axis runs over, the one named last changes fastest.
Arguments:
- references: bfloat16 [2, 8, 8, 32768], P(None, 'cls', None, ('dom', 'orient')), may hold values from -2 to 2
- images: bfloat16 [2, 2048, 32768], P(None, ('dom', 'orient')), may hold values from -16 to 16
- orient_lists: int32 [2048, 1], P(('dom', 'orient')), may hold values from 0 to 7; in each aligned block of 16 rows (0 to 15, 16 to 31, ...) at most 3 rows name the same one
- shift_ids: int32 [2048, 1], P(('dom', 'orient')), may hold values from 0 to 63
- fixed_weights: float32 [2048, 1], P(('dom', 'orient')), may hold values from 0.2 to 2
Outputs:
- class_prob: float32 [2048, 8], P(('dom', 'orient'), 'cls')
- volume: float32 [2, 8, 8, 32768], P(None, 'cls', 'orient', 'dom')
Inputs may be any that keep to these rules, and one draw needn't show every extreme that they name: `orient_lists`: within the rows of one device (16 particles), no orientation bin is listed by more than 3 particles, a bound that some block reaches.
All inputs are finite; a program needn't handle non-finite values.
Results may differ from a plain program's by a relative error of at most 0.02.
Values may be sent and summed in bfloat16 or wider, within the bound.
A program may use at most 320 MiB of HBM per device.

v0:
```python
import math

import jax
import jax.numpy as jnp
from jax import lax
from jax.sharding import PartitionSpec as P

IMG = 256
TX = 8
TY = 8


TWO_PI = 2.0 * math.pi


def freq_ids(columns):
    freq_x = (columns % IMG - IMG // 2).astype(jnp.float32)
    freq_y = (columns // IMG).astype(jnp.float32)
    return (freq_x, freq_y)


def offsets(number):
    return (jnp.arange(number, dtype=jnp.int32) - number // 2).astype(jnp.float32)


def local(references, images, orient_lists, shift_ids, fixed_weights):
    particles_here = images.shape[1]
    full_pixels = images.shape[2]
    class_here = references.shape[1]
    orient_here = references.shape[2]
    list_length = orient_lists.shape[1]
    entry_count = particles_here * list_length
    image_re = images[0]
    image_im = images[1]
    piece = lax.all_gather(references, ("dom", "orient"), axis=3, tiled=True)
    band_width = piece.shape[3]
    columns = jnp.arange(band_width, dtype=jnp.int32)
    freq_x, freq_y = freq_ids(columns)
    angle_x = TWO_PI / IMG * (offsets(TX)[:, None] * freq_x[None, :])
    angle_y = TWO_PI / IMG * (offsets(TY)[:, None] * freq_y[None, :])
    cosine_x = jnp.cos(angle_x)
    sine_x = jnp.sin(angle_x)
    cosine_y = jnp.cos(angle_y)
    sine_y = jnp.sin(angle_y)
    band_re = image_re.astype(jnp.float32)
    band_im = image_im.astype(jnp.float32)
    shifted_x_re = (
        (band_re[None] * cosine_x[:, None] - band_im[None] * sine_x[:, None])
        .astype(jnp.bfloat16)
        .reshape(TX * particles_here, band_width)
    )
    shifted_x_im = (
        (band_re[None] * sine_x[:, None] + band_im[None] * cosine_x[:, None])
        .astype(jnp.bfloat16)
        .reshape(TX * particles_here, band_width)
    )
    ref_re = piece[0].reshape(class_here * orient_here, band_width).astype(jnp.float32)
    ref_im = piece[1].reshape(class_here * orient_here, band_width).astype(jnp.float32)
    shifted_ref_re = (
        (ref_re[None] * cosine_y[:, None] + ref_im[None] * sine_y[:, None])
        .astype(jnp.bfloat16)
        .reshape(TY * class_here * orient_here, band_width)
    )
    shifted_ref_im = (
        (ref_im[None] * cosine_y[:, None] - ref_re[None] * sine_y[:, None])
        .astype(jnp.bfloat16)
        .reshape(TY * class_here * orient_here, band_width)
    )
    partial_value = jnp.einsum(
        "aj,bj->ab", shifted_x_re, shifted_ref_re, preferred_element_type=jnp.float32
    )
    partial_value = partial_value + jnp.einsum(
        "aj,bj->ab", shifted_x_im, shifted_ref_im, preferred_element_type=jnp.float32
    )
    logits = partial_value.reshape(TX, particles_here, TY, class_here, orient_here)
    local_top = jnp.max(logits, axis=(0, 2, 3, 4))
    global_top = lax.pmax(local_top, "cls")
    exponent = jnp.exp(logits - global_top[None, :, None, None, None])
    totals = lax.psum(jnp.sum(exponent, axis=(0, 2, 3, 4)), "cls")
    class_prob = jnp.sum(exponent, axis=(0, 2, 4)) / totals[:, None]
    orient_ids = orient_lists.reshape(entry_count)
    shift_index = shift_ids.reshape(entry_count)
    particle_of = jnp.arange(entry_count, dtype=jnp.int32) // list_length
    insert_weight = (
        (fixed_weights[:, :, None] * class_prob[:, None, :])
        .astype(jnp.bfloat16)
        .reshape(entry_count, class_here)
    )
    all_columns = jnp.arange(full_pixels, dtype=jnp.int32)
    freq_x_all, freq_y_all = freq_ids(all_columns)
    orient_range = jnp.arange(orient_here, dtype=jnp.int32)
    band_count = lax.axis_size("dom")
    slot_most = max(2, 3 * entry_count // (2 * orient_here))
    owner_hit = (orient_ids[:, None] == orient_range[None, :]).astype(jnp.int32)
    before = jnp.cumsum(owner_hit, axis=0) - owner_hit
    slot_place = jnp.sum(before * owner_hit, axis=1)
    slot_range = jnp.arange(slot_most, dtype=jnp.int32)
    slot_pick = owner_hit.T[:, None, :] * (
        slot_place[None, None, :] == slot_range[None, :, None]
    ).astype(jnp.int32)
    source = jnp.sum(
        slot_pick * jnp.arange(entry_count, dtype=jnp.int32)[None, None, :], axis=2
    ).reshape(orient_here * slot_most)
    filled = jnp.sum(slot_pick, axis=2).reshape(orient_here * slot_most)
    particle_pick = particle_of[source]
    shift_pick = shift_index[source]
    picked_re = image_re[particle_pick].astype(jnp.float32)
    picked_im = image_im[particle_pick].astype(jnp.float32)
    entry_x = (shift_pick % TX - TX // 2).astype(jnp.float32)
    entry_y = (shift_pick // TX - TY // 2).astype(jnp.float32)
    angle = (
        TWO_PI
        / IMG
        * (entry_x[:, None] * freq_x_all[None, :] + entry_y[:, None] * freq_y_all[None, :])
    )
    cosine = jnp.cos(angle)
    sine = jnp.sin(angle)
    row_re = (picked_re * cosine - picked_im * sine).astype(jnp.bfloat16)
    row_im = (picked_re * sine + picked_im * cosine).astype(jnp.bfloat16)
    row_re, row_im = (row_re, row_im)
    slot_weight = insert_weight[source] * filled[:, None].astype(jnp.bfloat16)
    stacked = jnp.stack([row_re, row_im], 1).reshape(
        orient_here, slot_most, 2, band_count, full_pixels // band_count
    )
    stacked = jnp.transpose(stacked, (3, 0, 1, 2, 4)).reshape(
        band_count * orient_here, slot_most, 2, full_pixels // band_count
    )
    slot_weight = jnp.broadcast_to(
        slot_weight.reshape(1, orient_here, slot_most, class_here),
        (band_count, orient_here, slot_most, class_here),
    ).reshape(band_count * orient_here, slot_most, class_here)
    arrived_rows, arrived_weights = (
        lax.all_to_all(stacked, ("dom", "orient"), split_axis=0, concat_axis=0, tiled=True),
        lax.all_to_all(slot_weight, ("dom", "orient"), split_axis=0, concat_axis=0, tiled=True),
    )
    volume = jnp.einsum(
        "smk,smrj->rkj", arrived_weights, arrived_rows, preferred_element_type=jnp.float32
    )[:, :, None, :]
    return (class_prob, volume)


def solution(mesh):
    in_specs = (
        P(None, "cls", None, ("dom", "orient")),
        P(None, ("dom", "orient"), None),
        P(("dom", "orient"), None),
        P(("dom", "orient"), None),
        P(("dom", "orient"), None),
    )
    out_specs = (P(("dom", "orient"), "cls"), P(None, "cls", "orient", "dom"))
    return jax.shard_map(local, mesh=mesh, in_specs=in_specs, out_specs=out_specs, check_vma=False)
```

profile of v0, /device:TPU:1, one launch (start us, length us, event | category | flops | bytes accessed | tf_op | source)
XLA Modules:
  0.0 472.0 jit_solution(16549917761253654394)
XLA Ops:
  7.2 0.0 copy-start
  7.2 0.0 all-gather.2.cloned.1.call-start
  7.2 0.7 all-gather.2.cloned.1.call-update
  7.9 0.7 fusion.14
  8.6 0.5 add_convert_fusion.3
  9.1 0.7 fusion.30
  9.8 0.7 fusion.35
  10.5 0.1 fusion.18
  10.6 0.0 copy-start.9
  10.6 4.0 slice_bitcast_fusion.3
  14.7 0.0 copy-done.9
  14.7 0.2 select_reduce_fusion
  14.9 0.2 multiply_reduce_fusion
  15.0 0.1 copy.50
  15.1 0.1 reshape.559
  15.2 0.1 copy.53
  15.3 0.7 gather_fusion
  16.1 2.8 gather_fusion.1
  18.8 4.1 copy.64
  22.9 1.6 gather_fusion.3
  24.5 2.6 copy.65
  27.1 0.0 copy-done
  27.1 1.2 gather_fusion.2
  28.3 0.7 gather.25
  29.0 9.5 %fusion.10 = (f32[8,32768]{1,0:T(8,128)}, f32[8,32768]{1,0:T(8,128)}, f32[8,32768]{1,0:T(8,128)S(1)}, f32[8,32768]{1,0:T(8,128)S(1)}) fusion(f32[32768]{0:T(1024)} %get-tuple-element.39, f32[8]{0:T(128)} %add_convert_fusion.3, f32[32768]{0:T(1024)S(1)} %get-tuple-element.38), kind=kLoop, calls=%fused_computation.26 | loop fusion | flops 1048576 | bytes 4456480 | tf_op jit(solution)/shard_map/cos | solution.py:43
  38.5 0.0 copy-done.2
  38.6 14.7 %subtract_convert_fusion.2 = (bf16[8,3,1,16,2048]{4,3,1,0,2:T(8,128)(2,1)}, bf16[8,3,1,16,2048]{4,3,1,0,2:T(8,128)(2,1)}) fusion(f32[8,3,1,16,2048]{4,3,1,0,2:T(8,128)} %bitcast.69, f32[8,3,1,16,2048]{4,3,1,0,2:T(8,128)S(1)} %bitcast.68, f32[16,2048]{1,0:T(8,128)S(1)} %get-tuple-element.41, f32[8,3]{1,0:T(8,128)S(1)} %get-tuple-element.33, ...), kind=kLoop, calls=%fused_computation.13 | loop fusion | flops 9437184 | bytes 9699520 | tf_op jit(solution)/shard_map/convert_element_type | solution.py:118
  53.3 0.0 copy-done.3
  53.3 7.1 %add_convert_fusion.1 = (bf16[8,16,32768]{2,1,0:T(8,128)(2,1)}, bf16[8,16,32768]{2,1,0:T(8,128)(2,1)}) fusion(f32[8,32768]{1,0:T(8,128)S(1)} %get-tuple-element.34, f32[16,32768]{1,0:T(8,128)S(1)} %copy-done.3, f32[8,32768]{1,0:T(8,128)S(1)} %get-tuple-element.35, f32[16,32768]{1,0:T(8,128)S(1)} %copy-done.4), kind=kLoop, calls=%fused_computation.7 | loop fusion | flops 33554432 | bytes 23068672 | tf_op jit(solution)/shard_map/convert_element_type | solution.py:54
  60.4 242.1 %all-gather.2.cloned.1.call-done = bf16[2,4,8,32768]{3,2,1,0:T(8,128)(2,1)} async-done(((bf16[2,4,8,256]{3,2,1,0:T(8,128)(2,1)}), bf16[2,4,8,32768]{3,2,1,0:T(8,128)(2,1)}) %all-gather.2.cloned.1.call-update) | async-done | bytes 4194320 | tf_op jit(solution)/shard_map/all_gather | solution.py:35
  302.5 2.8 fusion.8
  305.3 0.0 copy-done.7
  305.3 0.0 copy-done.8
  305.3 13.3 %subtract_convert_fusion = (bf16[8,32,32768]{2,1,0:T(8,128)(2,1)}, bf16[8,32,32768]{2,1,0:T(8,128)(2,1)}) fusion(f32[8,32768]{1,0:T(8,128)S(1)} %copy-done.8, f32[32,32768]{1,0:T(8,128)S(1)} %get-tuple-element.23, f32[8,32768]{1,0:T(8,128)S(1)} %copy-done.7, f32[32,32768]{1,0:T(8,128)S(1)} %get-tuple-element.22), kind=kLoop, calls=%fused_computation.5 | loop fusion | flops 67108864 | bytes 44040192 | tf_op jit(solution)/shard_map/convert_element_type | solution.py:66
  318.6 13.9 %fusion.45 = f32[128,256]{1,0:T(8,128)S(1)} fusion(bf16[128,32768]{1,0:T(8,128)(2,1)} %bitcast.66, bf16[256,32768]{1,0:T(8,128)(2,1)} %bitcast.64), kind=kOutput, calls=%fused_computation.94 | convolution fusion | flops 2147483648 | bytes 25296896 | tf_op jit(solution)/shard_map/aj,bj->ab/dot_general | solution.py:69
  332.4 0.0 copy-start.10
  332.5 13.9 %fusion.44 = (f32[128]{0:T(128)S(1)}, f32[128,256]{1,0:T(8,128)S(1)}) fusion(f32[128,256]{1,0:T(8,128)S(1)} %fusion.45, bf16[128,32768]{1,0:T(8,128)(2,1)} %bitcast.67, bf16[256,32768]{1,0:T(8,128)(2,1)} %bitcast.65), kind=kOutput, calls=%fused_computation.93 | convolution fusion | flops 2147549184 | bytes 25428480 | tf_op jit(solution)/shard_map/aj,bj->ab/dot_general | solution.py:72
  346.4 0.1 reduce_max.14
  346.5 5.6 %pmax.7 = f32[16]{0:T(128)S(1)} all-reduce(f32[16]{0:T(128)S(1)} %reduce_max.18), channel_id=1, replica_groups=mesh['cls'=2,'dom'=16,'orient'=8] {'cls'}, use_global_device_ids=true, to_apply=%region_2.3 | all-reduce | flops 16 | bytes 128 | tf_op jit(solution)/shard_map/pmax | solution.py:77
  352.1 0.1 sub.119
  352.2 0.1 copy.48
  352.3 0.2 exponential_reduce_fusion.1
  352.5 0.1 reduce_sum.54
  352.6 5.3 %psum.7 = f32[16]{0:T(128)S(1)} all-reduce(f32[16]{0:T(128)S(1)} %reduce_sum.55), channel_id=1, replica_groups=mesh['cls'=2,'dom'=16,'orient'=8] {'cls'}, use_global_device_ids=true, to_apply=%region_6.7 | all-reduce | flops 16 | bytes 128 | tf_op jit(solution)/shard_map/psum | solution.py:79
  357.9 1.3 reshape.558
  359.2 1.4 exponential_reduce_fusion
  360.6 0.1 copy.49
  360.7 0.1 multiply_convert_fusion
  360.8 0.6 gather_fusion.4
  361.3 0.1 copy.52
  361.4 0.1 gather.28
  361.5 0.2 copy.62
  361.7 0.7 broadcast_in_dim.4.clone
  362.4 10.2 %all-to-all-start.1 = ((bf16[128,3,4]{2,1,0:T(4,128)(2,1)}), bf16[128,3,4]{2,1,0:T(4,128)(2,1)S(1)}, u32[]{:S(2)}, u32[]{:S(2)}) async-start(bf16[128,3,4]{2,1,0:T(4,128)(2,1)} %bitcast.16), calls=%async_computation.1 | async-start | bytes 262144 | tf_op jit(solution)/shard_map/all_to_all | solution.py:134
  372.6 0.3 maximum_bitcast_fusion
  372.9 4.9 %copy.51 = bf16[16,8,3,2,2048]{4,3,2,1,0:T(2,128)(2,1)} copy(bf16[16,8,3,2,2048]{4,0,2,1,3:T(8,128)(2,1)S(1)} %maximum_bitcast_fusion) | data formatting | bytes 6291456 | tf_op jit(solution)/shard_map/transpose | solution.py:125
  377.8 6.0 %all-to-all-done.1 = bf16[128,3,4]{2,1,0:T(4,128)(2,1)S(1)} async-done(((bf16[128,3,4]{2,1,0:T(4,128)(2,1)}), bf16[128,3,4]{2,1,0:T(4,128)(2,1)S(1)}, u32[]{:S(2)}, u32[]{:S(2)}) %all-to-all-start.1) | async-done | bytes 3104 | tf_op jit(solution)/shard_map/all_to_all | solution.py:134
  383.8 6.7 %all-to-all-start = ((bf16[128,3,2,2048]{3,2,1,0:T(2,128)(2,1)}), bf16[128,3,2,2048]{3,2,1,0:T(2,128)(2,1)S(1)}, u32[]{:S(2)}, u32[]{:S(2)}) async-start(bf16[128,3,2,2048]{3,2,1,0:T(2,128)(2,1)} %bitcast.14), calls=%async_computation | async-start | bytes 6291456 | tf_op jit(solution)/shard_map/all_to_all | solution.py:133
  390.5 0.0 copy-start.1
  390.5 0.7 copy.58
  391.2 0.1 copy.57
  391.3 72.2 %all-to-all-done = bf16[128,3,2,2048]{3,2,1,0:T(2,128)(2,1)S(1)} async-done(((bf16[128,3,2,2048]{3,2,1,0:T(2,128)(2,1)}), bf16[128,3,2,2048]{3,2,1,0:T(2,128)(2,1)S(1)}, u32[]{:S(2)}, u32[]{:S(2)}) %all-to-all-start) | async-done | bytes 3145760 | tf_op jit(solution)/shard_map/all_to_all | solution.py:133
  463.5 0.9 fusion.4
  464.4 0.7 copy.59
  (25 shorter events, 0.2 us)
Async XLA Ops:
  7.2 19.9 %copy-start = (s32[16,1]{0,1:T(1,128)S(1)}, s32[16,1]{0,1:T(1,128)}, u32[]{:S(2)}) copy-start(s32[16,1]{0,1:T(1,128)} %param.8) | copy-start | bytes 196
  7.2 295.3 %all-gather.2.cloned.1.call-start = ((), (), s32[]{:S(2)}) async-start(), calls=%async_computation.2 | async-start | bytes 4227072 | tf_op jit(solution)/shard_map/all_gather | solution.py:35
  10.6 4.1 copy-start.9
  27.1 11.5 %copy-start.2 = (f32[3,8,16,2048]{3,2,1,0:T(8,128)S(1)}, f32[3,8,16,2048]{3,2,1,0:T(8,128)}, u32[]{:S(2)}) copy-start(f32[3,8,16,2048]{3,2,1,0:T(8,128)} %copy.64) | copy-start | bytes 9437188
  38.6 14.8 %copy-start.3 = (f32[16,32768]{1,0:T(8,128)S(1)}, f32[16,32768]{1,0:T(8,128)}, u32[]{:S(2)}) copy-start(f32[16,32768]{1,0:T(8,128)} %get-tuple-element.25) | copy-start | bytes 6291460
  38.6 14.8 %copy-start.4 = (f32[16,32768]{1,0:T(8,128)S(1)}, f32[16,32768]{1,0:T(8,128)}, u32[]{:S(2)}) copy-start(f32[16,32768]{1,0:T(8,128)} %get-tuple-element.26) | copy-start | bytes 6291460
  60.4 244.9 %copy-start.7 = (f32[8,32768]{1,0:T(8,128)S(1)}, f32[8,32768]{1,0:T(8,128)}, u32[]{:S(2)}) copy-start(f32[8,32768]{1,0:T(8,128)} %get-tuple-element.28) | copy-start | bytes 3145732
  60.4 244.9 %copy-start.8 = (f32[8,32768]{1,0:T(8,128)S(1)}, f32[8,32768]{1,0:T(8,128)}, u32[]{:S(2)}) copy-start(f32[8,32768]{1,0:T(8,128)} %get-tuple-element.29) | copy-start | bytes 3145732
  332.4 28.2 %copy-start.10 = (f32[16,1]{0,1:T(1,128)S(1)}, f32[16,1]{0,1:T(1,128)}, u32[]{:S(2)}) copy-start(f32[16,1]{0,1:T(1,128)} %param.9) | copy-start | bytes 196
  346.4 26.1 %copy-start.5 = (bf16[8,3,1,16,2048]{4,3,1,0,2:T(8,128)(2,1)S(1)}, bf16[8,3,1,16,2048]{4,3,1,0,2:T(8,128)(2,1)}, u32[]{:S(2)}) copy-start(bf16[8,3,1,16,2048]{4,3,1,0,2:T(8,128)(2,1)} %get-tuple-element.18) | copy-start | bytes 4718596
  346.4 26.1 %copy-start.6 = (bf16[8,3,1,16,2048]{4,3,1,0,2:T(8,128)(2,1)S(1)}, bf16[8,3,1,16,2048]{4,3,1,0,2:T(8,128)(2,1)}, u32[]{:S(2)}) copy-start(bf16[8,3,1,16,2048]{4,3,1,0,2:T(8,128)(2,1)} %get-tuple-element.19) | copy-start | bytes 4718596
  362.4 21.4 %all-to-all-start.1 = ((bf16[128,3,4]{2,1,0:T(4,128)(2,1)}), bf16[128,3,4]{2,1,0:T(4,128)(2,1)S(1)}, u32[]{:S(2)}, u32[]{:S(2)}) async-start(bf16[128,3,4]{2,1,0:T(4,128)(2,1)} %bitcast.16), calls=%async_computation.1 | async-start | bytes 262144 | tf_op jit(solution)/shard_map/all_to_all | solution.py:134
  383.8 79.7 %all-to-all-start = ((bf16[128,3,2,2048]{3,2,1,0:T(2,128)(2,1)}), bf16[128,3,2,2048]{3,2,1,0:T(2,128)(2,1)S(1)}, u32[]{:S(2)}, u32[]{:S(2)}) async-start(bf16[128,3,2,2048]{3,2,1,0:T(2,128)(2,1)} %bitcast.14), calls=%async_computation | async-start | bytes 6291456 | tf_op jit(solution)/shard_map/all_to_all | solution.py:133
  390.5 74.6 %copy-start.1 = (s32[16,1]{0,1:T(1,128)S(1)}, s32[16,1]{0,1:T(1,128)}, u32[]{:S(2)}) copy-start(s32[16,1]{0,1:T(1,128)} %param.8) | copy-start | bytes 196
Sparse Core Ops, SparseCore 0:
  9.8 292.6 all-gather.1
where the time goes:
time: 474 us; the launch traced here: 472 us
  waiting for transfers between devices  321 us (68%)
  other arithmetic  56.6 us (12%)
  matrix products  28.7 us (6%)
  local copies, waits for them, and re-layouts  23.6 us (5%)
  starting transfers between devices  16.9 us (4%)
  between operations  14.2 us (3%)
  blocking collectives  10.9 us (2%)
    all_gather x1, waiting for transfers between devices, local(): piece = lax.all_gather(references, ('dom', 'orient'), axis=3, tiled=True)  242 us
    all_to_all x1, waiting for transfers between devices, local(): lax.all_to_all(stacked, ('dom', 'orient'), split_axis=0, concat_axis=0, t...  72.2 us
    convert_element_type x1, other arithmetic, local(): row_re = (picked_re * cosine - picked_im * sine).astype(jnp.bfloat16)  14.7 us
    dot_general x1, matrix products, local(): jnp.einsum('aj,bj->ab', shifted_x_im, shifted_ref_im, preferred_element_t...  13.9 us
    dot_general x1, matrix products, local(): jnp.einsum('aj,bj->ab', shifted_x_re, shifted_ref_re, preferred_element_t...  13.9 us
    convert_element_type x1, other arithmetic, local(): shifted_ref_im = (ref_im[None] * cosine_y[:, None] - ref_re[None] * sine_...  13.3 us
    all_to_all x1, starting transfers between devices, local(): lax.all_to_all(slot_weight, ('dom', 'orient'), split_axis=0, concat_axis=...  10.2 us
    cos x1, other arithmetic, local(): cosine_y = jnp.cos(angle_y)  9.51 us
  transfers between devices with their start and end apart: 3, of which 3 were waited for; matrix products, arithmetic and copies ran while one was open for 12% of the time, Pallas kernels for 0%

commit v1 on v0

v1 whole, which is shorter than its diff:
```python
import math

import jax
import jax.numpy as jnp
from jax import lax
from jax.sharding import PartitionSpec as P

IMG = 256
TX = 8
TY = 8
TWO_PI = 2.0 * math.pi


def offsets(number):
    return (jnp.arange(number, dtype=jnp.int32) - number // 2).astype(jnp.float32)


def local(references, images, orient_lists, shift_ids, fixed_weights):
    here = images.shape[1]
    classes, orients = references.shape[1], references.shape[2]
    doms = lax.axis_size("dom")
    band = images.shape[2] // doms
    particles = here * doms
    held = lax.all_to_all(images, "dom", split_axis=2, concat_axis=1, tiled=True)
    piece = lax.all_gather(references, "orient", axis=3, tiled=True)
    ids = lax.all_gather(
        jnp.concatenate([orient_lists, shift_ids], axis=1), "dom", axis=0, tiled=True
    )
    orient_ids, shift_index = ids[:, 0], ids[:, 1]
    columns = jnp.arange(band, dtype=jnp.int32) + lax.axis_index("dom") * band
    freq_x = (columns % IMG - IMG // 2).astype(jnp.float32)
    freq_y = (columns // IMG).astype(jnp.float32)
    angle_x = TWO_PI / IMG * (offsets(TX)[:, None] * freq_x[None, :])
    angle_y = TWO_PI / IMG * (offsets(TY)[:, None] * freq_y[None, :])
    cx, sx, cy, sy = jnp.cos(angle_x), jnp.sin(angle_x), jnp.cos(angle_y), jnp.sin(angle_y)
    re, im = held[0].astype(jnp.float32), held[1].astype(jnp.float32)
    x_re = (re[:, None] * cx - im[:, None] * sx).astype(jnp.bfloat16).reshape(particles * TX, band)
    x_im = (re[:, None] * sx + im[:, None] * cx).astype(jnp.bfloat16).reshape(particles * TX, band)
    r_re = piece[0].reshape(classes * orients, band).astype(jnp.float32)
    r_im = piece[1].reshape(classes * orients, band).astype(jnp.float32)
    s_re = (r_re[None] * cy[:, None] + r_im[None] * sy[:, None]).astype(jnp.bfloat16)
    s_im = (r_im[None] * cy[:, None] - r_re[None] * sy[:, None]).astype(jnp.bfloat16)
    s_re = s_re.reshape(TY * classes * orients, band)
    s_im = s_im.reshape(TY * classes * orients, band)
    part = jnp.einsum("aj,bj->ab", x_re, s_re, preferred_element_type=jnp.float32)
    part = part + jnp.einsum("aj,bj->ab", x_im, s_im, preferred_element_type=jnp.float32)
    part = lax.all_to_all(
        part.reshape(doms, here * TX, -1), "dom", split_axis=0, concat_axis=0, tiled=True
    )
    logits = jnp.sum(part, axis=0).reshape(here, TX, TY, classes, orients)
    top = jnp.max(logits, axis=(1, 2, 3, 4))
    top = lax.pmax(top, "cls")
    exponent = jnp.exp(logits - top[:, None, None, None, None])
    sums = jnp.sum(exponent, axis=(1, 2, 4))
    totals = lax.psum(jnp.sum(sums, axis=1), "cls")
    class_prob = sums / totals[:, None]
    weight = (fixed_weights * class_prob).astype(jnp.bfloat16)
    weight = lax.all_gather(weight, "dom", axis=0, tiled=True)
    entry_x = (shift_index % TX - TX // 2).astype(jnp.float32)
    entry_y = (shift_index // TX - TY // 2).astype(jnp.float32)
    angle = TWO_PI / IMG * (entry_x[:, None] * freq_x[None] + entry_y[:, None] * freq_y[None])
    cosine, sine = jnp.cos(angle), jnp.sin(angle)
    row_re = (re * cosine - im * sine).astype(jnp.bfloat16)
    row_im = (re * sine + im * cosine).astype(jnp.bfloat16)
    onehot = (orient_ids[:, None] == jnp.arange(orients, dtype=jnp.int32)[None]).astype(jnp.bfloat16)
    mixing = (onehot[:, :, None] * weight[:, None, :]).reshape(particles, orients * classes)
    grown = [
        jnp.einsum("pm,pj->mj", mixing, row, preferred_element_type=jnp.float32).reshape(
            orients, 1, classes, band
        )
        for row in (row_re, row_im)
    ]
    grown = jnp.concatenate(grown, axis=1)
    grown = lax.all_to_all(grown, "orient", split_axis=0, concat_axis=0, tiled=True)
    volume = jnp.sum(grown, axis=0)[:, :, None, :]
    return (class_prob, volume)


def solution(mesh):
    in_specs = (
        P(None, "cls", None, ("dom", "orient")),
        P(None, ("dom", "orient"), None),
        P(("dom", "orient"), None),
        P(("dom", "orient"), None),
        P(("dom", "orient"), None),
    )
    out_specs = (P(("dom", "orient"), "cls"), P(None, "cls", "orient", "dom"))
    return jax.shard_map(local, mesh=mesh, in_specs=in_specs, out_specs=out_specs, check_vma=False)
```

time: 474 us -> 258 us (0.54)
  waiting for transfers between devices: 321 us -> 1.35 us
  blocking collectives: 10.9 us -> 115 us
  local copies, waits for them, and re-layouts: 23.6 us -> 97 us
  other arithmetic: 56.6 us -> 15 us
  matrix products: 28.7 us -> 8.47 us
  between operations: 14.2 us -> 0.83 us
    all_gather x1 -> x0, waiting for transfers between devices: 242 us -> none  [local(): piece = lax.all_gather(references, ('dom', 'orient'), axis=3, tiled=True)]
    all_gather x0 -> x3, blocking collectives: none -> 82.5 us  [the longest x1 40.1 us: local(): lax.all_gather(jnp.concatenate([orient_lists, shift_ids], axis=1), 'dom',...]
    all_to_all x2, waiting for transfers between devices: 78.3 us -> 1.35 us  [the longest x1 1.35 us: local(): lax.all_to_all(images, 'dom', split_axis=2, concat_axis=1, tiled=True)]
    unnamed x27 -> x15, local copies, waits for them, and re-layouts: 8.23 us -> 66.2 us
    convert_element_type x12 -> x7, other arithmetic: 40.2 us -> 10.9 us  [the longest x1 8.74 us: local(): row_re = (re * cosine - im * sine).astype(jnp.bfloat16)]
    all_to_all x1, local copies, waits for them, and re-layouts: 0.1 us -> 23.3 us  [local(): lax.all_to_all(images, 'dom', split_axis=2, concat_axis=1, tiled=True)]
    all_to_all x0 -> x1, blocking collectives: none -> 22.2 us  [local(): lax.all_to_all(grown, 'orient', split_axis=0, concat_axis=0, tiled=True)]
    dot_general x3 -> x4, matrix products: 28.7 us -> 8.47 us  [the longest x1 3.91 us: local(): jnp.einsum('aj,bj->ab', x_im, s_im, preferred_element_type=jnp.float32)]
  transfers between devices with their start and end apart: 3 -> 2, of which waited for: 3 -> 1; matrix products, arithmetic and copies ran while one was open for 12% -> 5% of each run, Pallas kernels for 0% -> 0%
where the time goes in v1:
time: 258 us; the launch traced here: 254 us
  blocking collectives  115 us (45%)
  local copies, waits for them, and re-layouts  97 us (38%)
  starting transfers between devices  15.7 us (6%)
  other arithmetic  15 us (6%)
  matrix products  8.47 us (3%)
    unnamed x15, local copies, waits for them, and re-layouts  66.2 us
    all_gather x1, blocking collectives, local(): lax.all_gather(jnp.concatenate([orient_lists, shift_ids], axis=1), 'dom',...  40.1 us
    all_gather x1, blocking collectives, local(): piece = lax.all_gather(references, 'orient', axis=3, tiled=True)  24.1 us
    all_to_all x1, local copies, waits for them, and re-layouts, local(): lax.all_to_all(images, 'dom', split_axis=2, concat_axis=1, tiled=True)  23.3 us
    all_to_all x1, blocking collectives, local(): lax.all_to_all(grown, 'orient', split_axis=0, concat_axis=0, tiled=True)  22.2 us
    all_gather x1, blocking collectives, local(): weight = lax.all_gather(weight, 'dom', axis=0, tiled=True)  18.2 us
    all_to_all x1, starting transfers between devices, local(): lax.all_to_all(part.reshape(doms, here * TX, -1), 'dom', split_axis=0, co...  8.77 us
    convert_element_type x1, other arithmetic, local(): row_re = (re * cosine - im * sine).astype(jnp.bfloat16)  8.74 us
  transfers between devices with their start and end apart: 2, of which 1 were waited for; matrix products, arithmetic and copies ran while one was open for 5% of the time, Pallas kernels for 0%

profile of v1, /device:TPU:1, one launch (start us, length us, event | category | flops | bytes accessed | tf_op | source)
XLA Modules:
  0.0 253.7 jit_solution(4576734842398924274)
XLA Ops:
  0.6 30.9 %copy.31 = bf16[2,16,32768]{1,0,2:T(2,128)(2,1)} copy(bf16[2,16,32768]{2,1,0:T(8,128)(2,1)} %param.6) | data formatting | bytes 4194304 | tf_op args[1]
  31.5 20.8 %reshape.408 = bf16[16,2,32768]{2,1,0:T(2,128)(2,1)} reshape(bf16[32768,2,16]{2,1,0:T(2,128)(2,1)} %bitcast.57) | data formatting | bytes 4194304
  52.3 0.0 copy-start.1
  52.3 7.0 %all-to-all-start = ((bf16[16,2,32768]{2,1,0:T(2,128)(2,1)}), bf16[16,2,32768]{2,1,0:T(2,128)(2,1)S(1)}, u32[]{:S(2)}, u32[]{:S(2)}) async-start(bf16[16,2,32768]{2,1,0:T(2,128)(2,1)} %reshape.408), calls=%async_computation | async-start | bytes 4194304 | tf_op jit(solution)/shard_map/all_to_all | solution.py:24
  59.3 0.0 copy-done.1
  59.3 24.1 %all_gather.9 = bf16[2,4,8,2048]{3,2,1,0:T(8,128)(2,1)S(1)} all-gather(bf16[2,4,8,256]{3,2,1,0:T(8,128)(2,1)S(1)} %copy-done.1), channel_id=1, replica_groups=mesh['cls'=2,'dom'=16,'orient'=8] {'orient'}, dimensions={3}, use_global_device_ids=true | all-gather | bytes 294912 | tf_op jit(solution)/shard_map/all_gather | solution.py:25
  83.5 0.5 fusion.24
  84.0 1.5 subtract_convert_fusion.2
  85.6 1.3 all-to-all-done
  86.9 14.4 %reshape.409 = bf16[32768,2,16]{2,1,0:T(2,128)(2,1)} reshape(bf16[16,2,32768]{2,1,0:T(2,128)(2,1)S(1)} %all-to-all-done) | data formatting | bytes 4194304
  101.3 23.3 %copy.45 = bf16[2,16,16,2048]{3,2,1,0:T(8,128)(2,1)S(1)} copy(bf16[2,16,16,2048]{1,0,3,2:T(2,128)(2,1)} %bitcast.56) | data formatting | bytes 4194304 | tf_op jit(solution)/shard_map/all_to_all | solution.py:24
  124.6 0.5 slice_convert_fusion.1
  125.2 1.2 copy.33
  126.4 0.0 copy-start
  126.4 1.2 copy.34
  127.6 0.0 copy-done
  127.6 2.8 %fusion.1 = f32[2048,256]{1,0:T(8,128)S(1)} fusion(bf16[256,2048]{1,0:T(8,128)(2,1)S(1)} %bitcast.68, f32[8,2048]{1,0:T(8,128)S(1)} %get-tuple-element.15, f32[256,2048]{1,0:T(8,128)S(1)} %bitcast.65, f32[8,2048]{1,0:T(8,128)S(1)} %get-tuple-element.14, f32[256,2048]{1,0:T(8,128)S(1)} %bitcast.63), kind=kOutput, calls=%fused_computation.3 | convolution fusion | flops 2164260864 | bytes 7471104 | tf_op jit(solution)/shard_map/aj,bj->ab/dot_general | solution.py:45
  130.4 3.9 %fusion.14 = f32[2048,256]{1,0:T(8,128)} fusion(f32[2048,256]{1,0:T(8,128)S(1)} %fusion.1, bf16[256,2048]{1,0:T(8,128)(2,1)S(1)} %bitcast.67, f32[8,2048]{1,0:T(8,128)S(1)} %get-tuple-element.15, f32[256,2048]{1,0:T(8,128)S(1)} %bitcast.66, f32[8,2048]{1,0:T(8,128)S(1)} %get-tuple-element.14, f32[256,2048]{1,0:T(8,128)S(1)} %bitcast.64), kind=kOutput, calls=%fused_computation.14 | convolution fusion | flops 2164785152 | bytes 9568256 | tf_op jit(solution)/shard_map/aj,bj->ab/dot_general | solution.py:46
  134.3 0.0 copy-start.3
  134.3 0.0 copy-start.4
  134.3 8.8 %all-to-all-start.1 = ((f32[16,128,256]{2,1,0:T(8,128)}), f32[16,128,256]{2,1,0:T(8,128)}, u32[]{:S(2)}, u32[]{:S(2)}) async-start(f32[16,128,256]{2,1,0:T(8,128)} %bitcast.62), calls=%async_computation.1 | async-start | bytes 4194304 | tf_op jit(solution)/shard_map/all_to_all | solution.py:47
  143.1 0.0 copy-done.3
  143.1 0.0 copy-done.4
  143.1 40.1 %all-gather = s32[16,16,2]{1,2,0:T(2,128)S(1)} all-gather(s32[1,16,2]{1,2,0:T(2,128)S(1)} %add_bitcast_fusion), channel_id=1, replica_groups=mesh['cls'=2,'dom'=16,'orient'=8] {'dom'}, dimensions={0}, use_global_device_ids=true | all-gather | bytes 2176 | tf_op jit(solution)/shard_map/all_gather | solution.py:26
  183.3 0.1 reshape.391
  183.4 0.1 mul.358
  183.5 0.1 copy.38
  183.5 0.1 mul.362
  183.6 0.1 copy.39
  183.7 8.7 %subtract_convert_fusion.1 = (bf16[1,16,16,2048]{3,1,2,0:T(8,128)(2,1)S(1)}, bf16[1,16,16,2048]{3,1,2,0:T(8,128)(2,1)S(1)}) fusion(f32[2048]{0:T(1024)S(1)} %get-tuple-element.23, f32[16,16]{0,1:T(8,128)S(1)} %copy.39, f32[2048]{0:T(1024)S(1)} %get-tuple-element.22, f32[16,16]{0,1:T(8,128)S(1)} %copy.38, bf16[2,16,16,2048]{3,1,2,0:T(8,128)(2,1)S(1)} %bitcast.59), kind=kLoop, calls=%fused_computation.18 | loop fusion | flops 7340032 | bytes 4212736 | tf_op jit(solution)/shard_map/convert_element_type | solution.py:63
  192.4 0.6 copy.40
  193.0 1.6 copy.42
  194.6 0.0 all-to-all-done.1
  194.6 1.7 reduce_sum.43
  196.3 0.1 copy.35
  196.4 0.1 reduce_max.10
  196.5 0.1 reduce_max.14
  196.6 0.1 reduce_max.18
  196.7 5.3 %pmax.7 = f32[16]{0:T(128)S(1)} all-reduce(f32[16]{0:T(128)S(1)} %reduce_max.18), channel_id=1, replica_groups=mesh['cls'=2,'dom'=16,'orient'=8] {'cls'}, use_global_device_ids=true, to_apply=%region_3.4 | all-reduce | flops 16 | bytes 128 | tf_op jit(solution)/shard_map/pmax | solution.py:52
  202.0 0.1 sub.78
  202.1 0.1 sub.79
  202.2 0.2 exponential_reduce_fusion.1
  202.4 0.1 reduce_sum.46
  202.5 0.1 reduce_sum.47
  202.6 5.3 %psum.7 = f32[16]{0:T(128)S(1)} all-reduce(f32[16]{0:T(128)S(1)} %reduce_sum.47), channel_id=1, replica_groups=mesh['cls'=2,'dom'=16,'orient'=8] {'cls'}, use_global_device_ids=true, to_apply=%region_7.8 | all-reduce | flops 16 | bytes 128 | tf_op jit(solution)/shard_map/psum | solution.py:55
  207.9 0.0 copy-start.2
  207.9 1.1 reshape.384
  209.0 0.5 exponential_reduce_fusion
  209.5 0.0 copy-done.2
  209.5 0.6 fusion.36
  210.1 18.2 %all-gather.1 = bf16[16,16,4]{1,2,0:T(4,128)(2,1)S(1)} all-gather(bf16[1,16,4]{1,2,0:T(4,128)(2,1)S(1)} %get-tuple-element.4), channel_id=1, replica_groups=mesh['cls'=2,'dom'=16,'orient'=8] {'dom'}, dimensions={0}, use_global_device_ids=true | all-gather | bytes 2176 | tf_op jit(solution)/shard_map/all_gather | solution.py:58
  228.4 0.1 reshape.393
  228.6 0.3 convolution_bitcast_fusion.1
  228.8 1.5 convolution_bitcast_fusion
  230.4 0.3 copy.44
  230.7 22.2 %all_to_all.25 = f32[8,2,4,2048]{3,2,1,0:T(4,128)S(1)} all-to-all(f32[8,2,4,2048]{3,2,1,0:T(4,128)S(1)} %copy.44), channel_id=1, replica_groups=mesh['cls'=2,'dom'=16,'orient'=8] {'orient'}, dimensions={0} | all-to-all | bytes 1048576 | tf_op jit(solution)/shard_map/all_to_all | solution.py:74
  253.0 0.1 reduce_sum.48
  253.1 0.7 broadcast_in_dim.2
  (13 shorter events, 0.2 us)
Async XLA Ops:
  52.3 7.0 %copy-start.1 = (bf16[2,4,8,256]{3,2,1,0:T(8,128)(2,1)S(1)}, bf16[2,4,8,256]{3,2,1,0:T(8,128)(2,1)}, u32[]{:S(2)}) copy-start(bf16[2,4,8,256]{3,2,1,0:T(8,128)(2,1)} %param.5) | copy-start | bytes 98308
  52.3 34.6 %all-to-all-start = ((bf16[16,2,32768]{2,1,0:T(2,128)(2,1)}), bf16[16,2,32768]{2,1,0:T(2,128)(2,1)S(1)}, u32[]{:S(2)}, u32[]{:S(2)}) async-start(bf16[16,2,32768]{2,1,0:T(2,128)(2,1)} %reshape.408), calls=%async_computation | async-start | bytes 4194304 | tf_op jit(solution)/shard_map/all_to_all | solution.py:24
  126.4 1.2 copy-start
  134.3 8.8 %copy-start.3 = (s32[16,1]{0,1:T(1,128)S(1)}, s32[16,1]{0,1:T(1,128)}, u32[]{:S(2)}) copy-start(s32[16,1]{0,1:T(1,128)} %param.8) | copy-start | bytes 196
  134.3 8.8 %copy-start.4 = (s32[16,1]{0,1:T(1,128)S(1)}, s32[16,1]{0,1:T(1,128)}, u32[]{:S(2)}) copy-start(s32[16,1]{0,1:T(1,128)} %param.7) | copy-start | bytes 196
  134.3 60.3 %all-to-all-start.1 = ((f32[16,128,256]{2,1,0:T(8,128)}), f32[16,128,256]{2,1,0:T(8,128)}, u32[]{:S(2)}, u32[]{:S(2)}) async-start(f32[16,128,256]{2,1,0:T(8,128)} %bitcast.62), calls=%async_computation.1 | async-start | bytes 4194304 | tf_op jit(solution)/shard_map/all_to_all | solution.py:47
  207.9 1.6 copy-start.2

commit v2 on v1

v2 whole, which is shorter than its diff:
```python
import functools
import math

import jax
import jax.numpy as jnp
import numpy as np
from jax import lax
from jax.experimental import pallas as pl
from jax.experimental.pallas import tpu as pltpu
from jax.sharding import PartitionSpec as P

IMG = 256
TX = 8
TY = 8
MESH = pl.DeviceIdType.MESH
F32 = jnp.float32
BF16 = jnp.bfloat16


def kernel(
    doms, zs, refs, imgs, xcos, xsin, ycos, ysin, oid, sid, fixed, prob_out, vol_out,
    ref_all, sib, out_rows, in_rows, xs, rs, acc, got, stat, stat_in, mix, mix_in, slab, slab_in,
    plane_s, plane_r, sib_s, sib_r, row_s, row_r, ring_s, ring_r, one_s, one_r, mix_s, mix_r, z_s, z_r,
):
    here = imgs.shape[1]
    band = imgs.shape[2] // doms
    lines = band // IMG
    half = doms // 2
    columns = refs.shape[1]
    classes = columns // zs
    me_d, me_z, me_c = lax.axis_index("dom"), lax.axis_index("orient"), lax.axis_index("cls")
    core, me_q = me_d % 2, me_d // 2
    twin = me_d + 1 - 2 * core
    other = 1 - me_c

    def send(src, dst, s, r, to):
        return pltpu.make_async_remote_copy(
            src_ref=src, dst_ref=dst, send_sem=s, recv_sem=r, device_id=to, device_id_type=MESH
        )

    barrier = pltpu.get_barrier_semaphore()

    @pl.loop(1, doms)
    def _(i):
        pl.semaphore_signal(barrier, inc=1, device_id={"dom": (me_d + i) % doms}, device_id_type=MESH)

    @pl.loop(1, zs)
    def _(i):
        pl.semaphore_signal(barrier, inc=1, device_id={"orient": (me_z + i) % zs}, device_id_type=MESH)

    pl.semaphore_signal(barrier, inc=1, device_id={"cls": other}, device_id_type=MESH)
    pl.semaphore_wait(barrier, doms + zs - 1)

    def plane_copy(i):
        return send(
            refs, ref_all.at[me_z, me_q], plane_s.at[i], plane_r.at[i],
            {"dom": 2 * ((me_q + i) % half) + core},
        )

    @pl.loop(1, half)
    def _(i):
        plane_copy(i).start()

    ref_all[me_z, me_q] = refs[...]

    def sib_copy(q):
        start = pl.multiple_of((2 * q + 1 - core) * band, band)
        return send(imgs.at[:, :, pl.ds(start, band)], sib.at[q], sib_s.at[q], sib_r.at[q], {"dom": twin})

    @pl.loop(0, half)
    def _(q):
        sib_copy(q).start()

    def row_copy(i):
        return send(
            out_rows.at[i], in_rows.at[:, me_d], row_s.at[i], row_r.at[i], {"dom": (me_d + i) % doms}
        )

    shift = jnp.broadcast_to(sid[...], (here, 128))
    at_x, at_y = shift & (TX - 1), shift >> 3
    twice = lambda v: jnp.concatenate([v, v], axis=1)
    wide_x = twice(at_x)
    px_c = jnp.zeros((here, IMG), F32)
    px_s = jnp.zeros((here, IMG), F32)
    for a in range(TX):
        px_c = jnp.where(wide_x == a, xcos[a : a + 1, :], px_c)
        px_s = jnp.where(wide_x == a, xsin[a : a + 1, :], px_s)

    @pl.loop(0, doms)
    def _(i):
        d = (me_d + i) % doms

        @pl.loop(0, lines)
        def _(r):
            col = pl.multiple_of(d * band + r * IMG, IMG)
            re = imgs[0, :, pl.ds(col, IMG)].astype(F32)
            im = imgs[1, :, pl.ds(col, IMG)].astype(F32)
            py_c = jnp.zeros((here, 128), F32)
            py_s = jnp.zeros((here, 128), F32)
            for b in range(TY):
                py_c = jnp.where(at_y == b, ycos[(d * lines + r) * TY + b], py_c)
                py_s = jnp.where(at_y == b, ysin[(d * lines + r) * TY + b], py_s)
            py_c, py_s = twice(py_c), twice(py_s)
            c = px_c * py_c - px_s * py_s
            s = px_s * py_c + px_c * py_s
            to = pl.ds(pl.multiple_of(r * IMG, IMG), IMG)
            out_rows[i, 0, :, to] = (re * c - im * s).astype(BF16)
            out_rows[i, 1, :, to] = (re * s + im * c).astype(BF16)

        @pl.when(i > 0)
        def _():
            row_copy(i).start()

    in_rows[:, me_d] = out_rows[0]

    acc[...] = jnp.zeros_like(acc)

    @pl.loop(1, half)
    def _(i):
        plane_copy(i).wait()

    low, high = pl.ds(0, half // 2), pl.ds(half // 2, half // 2)
    right, left = (me_z + 1) % zs, (me_z + zs - 1) % zs

    def ring_copy(way, s, part):
        block = (me_z + zs - s) % zs if way == 0 else (me_z + s) % zs
        at = ref_all.at[block, low if part == 0 else high]
        n = 2 * way + part
        return send(at, at, ring_s.at[n, s], ring_r.at[n, s], {"orient": right if way == 0 else left})

    def correlate(block, q):
        d = 2 * q + core
        col = pl.multiple_of(d * band + block * IMG, IMG)
        near = pl.ds(pl.multiple_of(block * IMG, IMG), IMG)
        for n in range(2):
            if n == 0:
                re, im = imgs[0, :, pl.ds(col, IMG)], imgs[1, :, pl.ds(col, IMG)]
            else:
                re, im = sib[q, 0, :, near], sib[q, 1, :, near]
            row = n * TX * here
            mid = row + TX // 2 * here
            xs[mid : mid + here, 0:IMG] = re
            xs[mid : mid + here, IMG:] = im
            re, im = re.astype(F32), im.astype(F32)
            for t in range(1, TX // 2 + 1):
                a = TX // 2 - t
                co, si = xcos[a : a + 1, :], xsin[a : a + 1, :]
                rc, rsn, ic, isn = re * co, re * si, im * co, im * si
                at = row + a * here
                xs[at : at + here, 0:IMG] = (rc - isn).astype(BF16)
                xs[at : at + here, IMG:] = (rsn + ic).astype(BF16)
                if t < TX // 2:
                    at = row + (TX // 2 + t) * here
                    xs[at : at + here, 0:IMG] = (rc + isn).astype(BF16)
                    xs[at : at + here, IMG:] = (ic - rsn).astype(BF16)
        re, im = ref_all[block, q, 0], ref_all[block, q, 1]
        mid = TY // 2 * columns
        rs[mid : mid + columns, 0:IMG] = re
        rs[mid : mid + columns, IMG:] = im
        re, im = re.astype(F32), im.astype(F32)
        ky = (d * lines + block) * TY
        for t in range(1, TY // 2 + 1):
            b = TY // 2 - t
            co, si = ycos[ky + b], ysin[ky + b]
            rc, rsn, ic, isn = re * co, re * si, im * co, im * si
            at = b * columns
            rs[at : at + columns, 0:IMG] = (rc + isn).astype(BF16)
            rs[at : at + columns, IMG:] = (ic - rsn).astype(BF16)
            if t < TY // 2:
                at = (TY // 2 + t) * columns
                rs[at : at + columns, 0:IMG] = (rc - isn).astype(BF16)
                rs[at : at + columns, IMG:] = (ic + rsn).astype(BF16)
        acc[...] += lax.dot_general(
            xs[...], rs[...], (((1,), (1,)), ((), ())), preferred_element_type=F32
        )

    @pl.loop(0, half)
    def _(q):
        sib_copy(q).wait()

    steps = zs // 2

    @pl.loop(0, steps + 1)
    def _(s):
        @pl.when(s < steps)
        def _():
            ring_copy(0, s, 0).start()
            ring_copy(1, s, 1).start()

        @pl.when(s < steps - 1)
        def _():
            ring_copy(0, s, 1).start()
            ring_copy(1, s, 0).start()

        blocks = jnp.where((s == 0) | (s == steps), half, 2 * half)

        @pl.loop(0, blocks)
        def _(j):
            block = jnp.where(j < half, me_z + zs - s, me_z + s) % zs
            correlate(block, j % half)

        @pl.when(s < steps)
        def _():
            ring_copy(0, s, 0).wait()
            ring_copy(1, s, 1).wait()

        @pl.when(s < steps - 1)
        def _():
            ring_copy(0, s, 1).wait()
            ring_copy(1, s, 0).wait()

    rows = TX * here
    swap = send(acc.at[pl.ds(rows, rows)], got, one_s.at[0], one_r.at[0], {"dom": twin})
    swap.start()
    swap.wait()
    logits = (acc[0:rows] + got[...]).reshape(TX, here, TY * columns)
    top = jnp.max(jnp.max(logits, axis=0), axis=1, keepdims=True)
    grown = jnp.sum(jnp.exp(logits - top[None]), axis=0)
    lane = lax.broadcasted_iota(jnp.int32, (here, TY * columns), 1)
    of_class = (lane // zs) % classes
    sums = [jnp.sum(jnp.where(of_class == k, grown, 0.0), axis=1, keepdims=True) for k in range(classes)]
    total = sums[0]
    for k in range(1, classes):
        total = total + sums[k]
    lane = lax.broadcasted_iota(jnp.int32, (here, 128), 1)
    stat[...] = jnp.where(lane == 0, top, total)
    pair = send(stat, stat_in, one_s.at[1], one_r.at[1], {"cls": other})
    pair.start()
    pair.wait()
    top_in, total_in = stat_in[:, 0:1], stat_in[:, 1:2]
    both = jnp.maximum(top, top_in)
    scale = jnp.exp(top - both)
    total = total * scale + total_in * jnp.exp(top_in - both)
    probs = [sums[k] * scale / total for k in range(classes)]

    value = jnp.zeros((here, 128), F32)
    for k in range(classes):
        prob_out[:, k : k + 1] = probs[k]
        value = jnp.where(lane % classes == k, (fixed[...] * probs[k]).astype(BF16).astype(F32), value)
    wide = 2 * classes
    hit = ((lane // classes) % 2 == lane // (wide * zs)) & ((lane // wide) % zs == oid[...])
    mix[...] = jnp.where(hit, value, 0.0).astype(BF16)

    def mix_copy(i):
        return send(mix, mix_in.at[me_d], mix_s.at[i], mix_r.at[i], {"dom": (me_d + i) % doms})

    @pl.loop(1, doms)
    def _(i):
        mix_copy(i).start()

    mix_in[me_d] = mix[...]

    @pl.loop(1, doms)
    def _(i):
        row_copy(i).wait()

    @pl.loop(1, doms)
    def _(i):
        mix_copy(i).wait()

    turned = mix_in[...].reshape(doms * here, 128).astype(F32).T.astype(BF16)
    count = wide * zs
    part = jnp.dot(
        turned[0:count], in_rows[0].reshape(doms * here, band), preferred_element_type=F32
    ) + jnp.dot(turned[count:], in_rows[1].reshape(doms * here, band), preferred_element_type=F32)
    for o in range(zs):
        slab[o] = part[o * wide : (o + 1) * wide].astype(BF16)

    def z_copy(i):
        return send(slab.at[(me_z + i) % zs], slab_in.at[i], z_s.at[i], z_r.at[i], {"orient": (me_z + i) % zs})

    @pl.loop(1, zs)
    def _(i):
        z_copy(i).start()

    slab_in[0] = slab[me_z]

    @pl.loop(1, zs)
    def _(i):
        z_copy(i).wait()

    out = slab_in[0].astype(F32)
    for i in range(1, zs):
        out = out + slab_in[i].astype(F32)
    vol_out[...] = out


def tables():
    kx = np.arange(IMG) - IMG // 2
    ky = np.arange(IMG // 2)
    turn_x = 2 * np.pi / IMG * ((np.arange(TX) - TX // 2)[:, None] * kx[None, :])
    turn_y = 2 * np.pi / IMG * (ky[:, None] * (np.arange(TY) - TY // 2)[None, :])
    return [
        f(t).astype(np.float32) for t in (turn_x, turn_y.reshape(-1)) for f in (np.cos, np.sin)
    ]


def solution(mesh):
    doms, zs = mesh.shape["dom"], mesh.shape["orient"]

    def local(references, images, orient_lists, shift_ids, fixed_weights):
        classes, here = references.shape[1], images.shape[1]
        columns = classes * references.shape[2]
        band = images.shape[2] // doms
        half = doms // 2
        vmem, smem = pl.BlockSpec(memory_space=pltpu.VMEM), pl.BlockSpec(memory_space=pltpu.SMEM)
        dma = pltpu.SemaphoreType.DMA
        rows = TX * here
        prob, volume = pl.pallas_call(
            functools.partial(kernel, doms, zs),
            out_shape=(
                jax.ShapeDtypeStruct((here, classes), F32),
                jax.ShapeDtypeStruct((2 * classes, band), F32),
            ),
            in_specs=[vmem] * 4 + [smem] * 2 + [vmem] * 3,
            out_specs=(vmem, vmem),
            scratch_shapes=[
                pltpu.VMEM((zs, half, 2, columns, IMG), BF16),
                pltpu.VMEM((half, 2, here, band), BF16),
                pltpu.VMEM((doms, 2, here, band), BF16),
                pltpu.VMEM((2, doms, here, band), BF16),
                pltpu.VMEM((2 * rows, 2 * IMG), BF16),
                pltpu.VMEM((TY * columns, 2 * IMG), BF16),
                pltpu.VMEM((2 * rows, TY * columns), F32),
                pltpu.VMEM((rows, TY * columns), F32),
                pltpu.VMEM((here, 128), F32),
                pltpu.VMEM((here, 128), F32),
                pltpu.VMEM((here, 128), BF16),
                pltpu.VMEM((doms, here, 128), BF16),
                pltpu.VMEM((zs, 2 * classes, band), BF16),
                pltpu.VMEM((zs, 2 * classes, band), BF16),
                dma((half,)), dma((half,)),
                dma((half,)), dma((half,)),
                dma((doms,)), dma((doms,)),
                dma((4, zs // 2)), dma((4, zs // 2)),
                dma((2,)), dma((2,)),
                dma((doms,)), dma((doms,)),
                dma((zs,)), dma((zs,)),
            ],
            compiler_params=pltpu.CompilerParams(
                collective_id=0, has_side_effects=True, vmem_limit_bytes=40 << 20
            ),
            name="estep",
        )(
            references.reshape(2, columns, references.shape[3]),
            images,
            *[jnp.asarray(t) for t in tables()],
            orient_lists,
            shift_ids,
            fixed_weights,
        )
        return prob, volume.reshape(2, classes, 1, band)

    in_specs = (
        P(None, "cls", None, ("dom", "orient")),
        P(None, ("dom", "orient"), None),
        P(("dom", "orient"), None),
        P(("dom", "orient"), None),
        P(("dom", "orient"), None),
    )
    out_specs = (P(("dom", "orient"), "cls"), P(None, "cls", "orient", "dom"))
    return jax.shard_map(local, mesh=mesh, in_specs=in_specs, out_specs=out_specs, check_vma=False)
```

time: 258 us -> 79.8 us (0.31); the launches traced: 254 us -> 79.5 us
  blocking collectives: 115 us -> 0 us
  local copies, waits for them, and re-layouts: 97 us -> 8.67 us
  Pallas kernels: 0 us -> 70.1 us
  starting transfers between devices: 15.7 us -> 0 us
  other arithmetic: 15 us -> 0 us
  matrix products: 8.47 us -> 0 us
    all_gather x3 -> x0, blocking collectives: 82.5 us -> none  [the longest x1 40.1 us: local(): lax.all_gather(jnp.concatenate([orient_lists, shift_ids], axis=1), 'dom',...]
    pallas_call x0 -> x1, Pallas kernels: none -> 70.1 us  [local(): pl.pallas_call(functools.partial(kernel, doms, zs), out_shape=(jax.ShapeD...]
    unnamed x15 -> x16, local copies, waits for them, and re-layouts: 66.2 us -> 7.96 us
    all_to_all x1 -> x0, local copies, waits for them, and re-layouts: 23.3 us -> none  [local(): lax.all_to_all(images, 'dom', split_axis=2, concat_axis=1, tiled=True)]
    all_to_all x1 -> x0, blocking collectives: 22.2 us -> none  [local(): lax.all_to_all(grown, 'orient', split_axis=0, concat_axis=0, tiled=True)]
    all_to_all x2 -> x0, starting transfers between devices: 15.7 us -> none  [the longest x1 8.77 us: local(): lax.all_to_all(part.reshape(doms, here * TX, -1), 'dom', split_axis=0, co...]
    convert_element_type x8 -> x0, other arithmetic: 10.9 us -> none  [the longest x1 8.74 us: local(): row_re = (re * cosine - im * sine).astype(jnp.bfloat16)]
    dot_general x4 -> x0, matrix products: 8.47 us -> none  [the longest x1 3.91 us: local(): jnp.einsum('aj,bj->ab', x_im, s_im, preferred_element_type=jnp.float32)]
  transfers between devices with their start and end apart: 2 -> 0, of which waited for: 1 -> 0; matrix products, arithmetic and copies ran while one was open for 5% -> 0% of each run, Pallas kernels for 0% -> 0%
where the time goes in v2:
time: 79.8 us; the launch traced here: 79.5 us
  Pallas kernels  70.1 us (88%)
  local copies, waits for them, and re-layouts  8.67 us (11%)
    pallas_call x1, Pallas kernels, local(): pl.pallas_call(functools.partial(kernel, doms, zs), out_shape=(jax.ShapeD...  70.1 us
    unnamed x16, local copies, waits for them, and re-layouts  7.96 us

profile of v2, /device:TPU:1, one launch (start us, length us, event | category | flops | bytes accessed | tf_op | source)
XLA Modules:
  0.0 79.5 jit_solution(3333162847740399134)
XLA Ops:
  0.6 0.7 copy.11.oid
  1.4 0.7 copy.12.sid
  2.1 0.7 copy.13.fixed
  2.8 0.0 copy-start
  2.8 1.6 %copy-done = bf16[2,16,32768]{2,1,0:T(8,128)(2,1)S(1)} copy-done((bf16[2,16,32768]{2,1,0:T(8,128)(2,1)S(1)}, bf16[2,16,32768]{2,1,0:T(8,128)(2,1)}, u32[]{:S(2)}) %copy-start) | copy-done | bytes 2097176
  4.4 0.0 copy-start.1
  4.4 0.8 copy-done.1
  5.2 0.0 copy-start.2
  5.2 0.7 copy-done.2
  5.9 0.0 copy-start.3
  5.9 0.7 copy-done.3
  6.6 0.0 copy-start.4
  6.6 0.7 copy-done.4
  7.3 0.0 copy-start.5
  7.3 0.7 copy-done.5
  7.9 70.1 %estep.1 = (f32[16,4]{1,0:T(8,128)S(1)}, f32[8,2048]{1,0:T(8,128)S(1)}) custom-call(bf16[2,32,256]{2,1,0:T(8,128)(2,1)S(1)} %bitcast.1, bf16[2,16,32768]{2,1,0:T(8,128)(2,1)S(1)} %copy-done, f32[8,256]{1,0:T(8,128)S(1)} %copy-done.3, f32[8,256]{1,0:T(8,128)S(1)} %copy-done.2, f32[1024]{0:T(1024)S(1)} %copy-done.5, f32[1024]{0:T(1024)S(1)} %copy-done.4, ...), custom_call_target="tpu_custom_call" | custom-call | tf_op jit(solution)/shard_map/estep/pallas_call | solution.py:309
  78.1 0.7 copy.14
  78.7 0.7 reshape.12
Async XLA Ops:
  2.8 1.6 %copy-start = (bf16[2,16,32768]{2,1,0:T(8,128)(2,1)S(1)}, bf16[2,16,32768]{2,1,0:T(8,128)(2,1)}, u32[]{:S(2)}) copy-start(bf16[2,16,32768]{2,1,0:T(8,128)(2,1)} %imgs.1) | copy-start | bytes 6291460
  4.4 0.8 copy-start.1
  5.2 0.7 copy-start.2
  5.9 0.7 copy-start.3
  6.6 0.7 copy-start.4
  7.3 0.7 copy-start.5

commit v3 on v2

v3 whole, which is shorter than its diff:
```python
import functools
import math

import jax
import jax.numpy as jnp
import numpy as np
from jax import lax
from jax.experimental import pallas as pl
from jax.experimental.pallas import tpu as pltpu
from jax.sharding import PartitionSpec as P

IMG = 256
TX = 8
TY = 8
MESH = pl.DeviceIdType.MESH
F32 = jnp.float32
BF16 = jnp.bfloat16


def kernel(
    doms, zs, refs, images, xtab_in, ytab_in, oid_in, sid_in, fixed_in, prob_out, vol_out,
    imgs, xtab, ytab, oid_row, sid_row, fixed_row,
    ref_all, sib, out_rows, in_rows, xs_a, rs_a, xs_b, rs_b, acc, got, stat, pair_in, mix, mix_in, slab, slab_in,
    plane_s, plane_r, sib_s, sib_r, row_s, row_r, ring_s, ring_r, one_s, one_r, mix_s, mix_r, z_s, z_r, in_s,
):
    here = images.shape[1]
    band = images.shape[2] // doms
    lines = band // IMG
    half = doms // 2
    side = half // 2
    columns = refs.shape[1]
    classes = columns // zs
    steps = zs // 2
    me_d, me_z, me_c = lax.axis_index("dom"), lax.axis_index("orient"), lax.axis_index("cls")
    core, me_q = me_d % 2, me_d // 2
    me_x, me_l = me_q % side, me_q // side
    me_y = 2 * me_c + me_l
    twin = me_d + 1 - 2 * core
    other = 1 - me_c

    def send(src, dst, s, r, to):
        return pltpu.make_async_remote_copy(
            src_ref=src, dst_ref=dst, send_sem=s, recv_sem=r, device_id=to, device_id_type=MESH
        )

    barrier = pltpu.get_barrier_semaphore()

    def greet(to):
        pl.semaphore_signal(barrier, inc=1, device_id=to, device_id_type=MESH)

    @pl.loop(1, doms)
    def _(i):
        greet({"dom": (me_d + i) % doms})

    @pl.loop(1, zs)
    def _(i):
        greet({"orient": (me_z + i) % zs})

    greet({"cls": other})

    @pl.loop(0, half)
    def _(i):
        greet({"dom": half * (1 - me_l) + i, "cls": other})

    loads = [
        pltpu.make_async_copy(src, dst, in_s.at[n])
        for n, (src, dst) in enumerate(
            (
                (refs, ref_all.at[me_z, me_q]),
                (images, imgs),
                (xtab_in, xtab),
                (ytab_in, ytab),
                (oid_in, oid_row),
                (sid_in, sid_row),
                (fixed_in, fixed_row),
            )
        )
    ]
    for load in loads:
        load.start()
    pl.semaphore_wait(barrier, doms + zs - 1 + half)

    def plane_copy(j):
        to = (me_l + j // side) % 2 * side + (me_x + j % side) % side
        at = ref_all.at[me_z, me_q]
        return send(at, at, plane_s.at[j], plane_r.at[j], {"dom": 2 * to + core})

    def piece(j):
        return (me_l + j // side) % 2 * side + (me_x + side - j % side) % side

    def sib_copy(q):
        start = pl.multiple_of((2 * q + 1 - core) * band, band)
        return send(images.at[:, :, pl.ds(start, band)], sib.at[q], sib_s.at[q], sib_r.at[q], {"dom": twin})

    right, left = (me_z + 1) % zs, (me_z + zs - 1) % zs

    def ring_copy(way, s, j):
        block = (me_z + zs + 1 - s) % zs if way == 0 else (me_z + s - 1) % zs
        at = ref_all.at[block, piece(j)]
        return send(
            at, at, ring_s.at[way, s - 1, j], ring_r.at[way, s - 1, j], {"orient": right if way == 0 else left}
        )

    loads[0].wait()
    ring_copy(0, 1, 0).start()
    ring_copy(1, 1, 0).start()

    @pl.loop(1, half)
    def _(j):
        plane_copy(j).start()

    @pl.loop(0, half)
    def _(q):
        sib_copy(q).start()

    for load in loads[1:]:
        load.wait()

    xcos, xsin = xtab.at[0], xtab.at[1]
    ycos, ysin = (lambda n: ytab[0, n]), (lambda n: ytab[1, n])
    diagonal = lax.broadcasted_iota(jnp.int32, (here, here), 0) == lax.broadcasted_iota(
        jnp.int32, (here, here), 1
    )

    def column(row):
        wide = jnp.broadcast_to(row[...].astype(F32), (here, here))
        return jnp.sum(jnp.where(diagonal, wide, 0.0), axis=1, keepdims=True)

    oid, sid, fixed = column(oid_row).astype(jnp.int32), column(sid_row).astype(jnp.int32), column(fixed_row)
    shift = jnp.broadcast_to(sid, (here, 128))
    at_x, at_y = shift & (TX - 1), shift >> 3
    twice = lambda v: jnp.concatenate([v, v], axis=1)
    wide_x = twice(at_x)
    px_c = jnp.zeros((here, IMG), F32)
    px_s = jnp.zeros((here, IMG), F32)
    for a in range(TX):
        px_c = jnp.where(wide_x == a, xcos[a : a + 1, :], px_c)
        px_s = jnp.where(wide_x == a, xsin[a : a + 1, :], px_s)

    def band_of(i):
        return 2 * ((me_l + i // half) % 2 * side + (me_x + i // 2 % side) % side) + (core + i % 2) % 2

    def row_copy(i):
        return send(out_rows.at[i], in_rows.at[:, me_d], row_s.at[i], row_r.at[i], {"dom": band_of(i)})

    def part_copy(i, r):
        n = i + r * half
        y = (me_y + (1 if r == 0 else 3)) % 4
        return send(
            out_rows.at[i, r], in_rows.at[r, me_d], row_s.at[n], row_r.at[n], {"dom": band_of(i), "cls": y // 2}
        )

    @pl.loop(0, doms)
    def _(i):
        d = band_of(i)

        @pl.loop(0, lines)
        def _(r):
            col = pl.multiple_of(d * band + r * IMG, IMG)
            re = imgs[0, :, pl.ds(col, IMG)].astype(F32)
            im = imgs[1, :, pl.ds(col, IMG)].astype(F32)
            py_c = jnp.zeros((here, 128), F32)
            py_s = jnp.zeros((here, 128), F32)
            for b in range(TY):
                py_c = jnp.where(at_y == b, ycos((d * lines + r) * TY + b), py_c)
                py_s = jnp.where(at_y == b, ysin((d * lines + r) * TY + b), py_s)
            py_c, py_s = twice(py_c), twice(py_s)
            c = px_c * py_c - px_s * py_s
            s = px_s * py_c + px_c * py_s
            to = pl.ds(pl.multiple_of(r * IMG, IMG), IMG)
            out_rows[i, 0, :, to] = (re * c - im * s).astype(BF16)
            out_rows[i, 1, :, to] = (re * s + im * c).astype(BF16)

        @pl.when((i > 0) & (i < half))
        def _():
            row_copy(i).start()

        @pl.when(i >= half)
        def _():
            part_copy(i, 0).start()
            part_copy(i, 1).start()

    in_rows[:, me_d] = out_rows[0]

    acc[...] = jnp.zeros_like(acc)
    xs_b[...] = jnp.zeros_like(xs_b)
    rs_b[...] = jnp.zeros_like(rs_b)

    def prepare(xs, rs, block, q):
        d = 2 * q + core
        col = pl.multiple_of(d * band + block * IMG, IMG)
        near = pl.ds(pl.multiple_of(block * IMG, IMG), IMG)
        for n in range(2):
            if n == 0:
                re, im = imgs[0, :, pl.ds(col, IMG)], imgs[1, :, pl.ds(col, IMG)]
            else:
                re, im = sib[q, 0, :, near], sib[q, 1, :, near]
            row = n * TX * here
            mid = row + TX // 2 * here
            xs[mid : mid + here, 0:IMG] = re
            xs[mid : mid + here, IMG:] = im
            re, im = re.astype(F32), im.astype(F32)
            for t in range(1, TX // 2 + 1):
                a = TX // 2 - t
                co, si = xcos[a : a + 1, :], xsin[a : a + 1, :]
                rc, rsn, ic, isn = re * co, re * si, im * co, im * si
                at = row + a * here
                xs[at : at + here, 0:IMG] = (rc - isn).astype(BF16)
                xs[at : at + here, IMG:] = (rsn + ic).astype(BF16)
                if t < TX // 2:
                    at = row + (TX // 2 + t) * here
                    xs[at : at + here, 0:IMG] = (rc + isn).astype(BF16)
                    xs[at : at + here, IMG:] = (ic - rsn).astype(BF16)
        re, im = ref_all[block, q, 0], ref_all[block, q, 1]
        mid = TY // 2 * columns
        rs[mid : mid + columns, 0:IMG] = re
        rs[mid : mid + columns, IMG:] = im
        re, im = re.astype(F32), im.astype(F32)
        ky = (d * lines + block) * TY
        for t in range(1, TY // 2 + 1):
            b = TY // 2 - t
            co, si = ycos(ky + b), ysin(ky + b)
            rc, rsn, ic, isn = re * co, re * si, im * co, im * si
            at = b * columns
            rs[at : at + columns, 0:IMG] = (rc + isn).astype(BF16)
            rs[at : at + columns, IMG:] = (ic - rsn).astype(BF16)
            if t < TY // 2:
                at = (TY // 2 + t) * columns
                rs[at : at + columns, 0:IMG] = (rc - isn).astype(BF16)
                rs[at : at + columns, IMG:] = (ic + rsn).astype(BF16)

    def add(xs, rs):
        acc[...] += lax.dot_general(
            xs[...], rs[...], (((1,), (1,)), ((), ())), preferred_element_type=F32
        )

    @pl.loop(0, half)
    def _(q):
        sib_copy(q).wait()

    first, middle = half // 2, half * (steps - 1)

    @pl.loop(0, half + middle)
    def _(t):
        @pl.when(t < first)
        def _():
            for n in range(2):
                j = 2 * t + n

                @pl.when(j > 0)
                def _():
                    plane_copy(j).wait_recv()
                    ring_copy(0, 1, j).start()
                    ring_copy(1, 1, j).start()

        @pl.when((t >= first) & (t < first + middle))
        def _():
            s, j = 1 + (t - first) // half, (t - first) % half
            ring_copy(0, s, j).wait_recv()

            @pl.when((s < steps - 1) | (j < half // 2))
            def _():
                ring_copy(0, s + 1, j).start()

            ring_copy(1, s, j).wait_recv()

            @pl.when((s < steps - 1) | (j >= half // 2))
            def _():
                ring_copy(1, s + 1, j).start()

        @pl.when(t >= first + middle)
        def _():
            j = t - first - middle
            ring_copy(0, steps, j).wait_recv()
            ring_copy(1, steps, j + half // 2).wait_recv()

        at_first, at_last = t < first, t >= first + middle
        s, j = 1 + (t - first) // half, (t - first) % half
        near = jnp.where(at_last, steps, jnp.where(at_first, 0, s))
        j_a = jnp.where(at_last, t - first - middle, jnp.where(at_first, 2 * t, j))
        j_b = jnp.where(at_last, j_a + half // 2, jnp.where(at_first, 2 * t + 1, j))
        prepare(xs_a, rs_a, (me_z + zs - near) % zs, piece(j_a))
        add(xs_b, rs_b)
        prepare(xs_b, rs_b, (me_z + near) % zs, piece(j_b))
        add(xs_a, rs_a)

    add(xs_b, rs_b)

    rows = TX * here
    swap = send(acc.at[pl.ds(rows, rows)], got, one_s.at[0], one_r.at[0], {"dom": twin})
    swap.start()
    swap.wait()
    logits = (acc[0:rows] + got[...]).reshape(TX, here, TY * columns)
    top = jnp.max(jnp.max(logits, axis=0), axis=1, keepdims=True)
    grown = jnp.sum(jnp.exp(logits - top[None]), axis=0)
    lane = lax.broadcasted_iota(jnp.int32, (here, TY * columns), 1)
    of_class = (lane // zs) % classes
    sums = [jnp.sum(jnp.where(of_class == k, grown, 0.0), axis=1, keepdims=True) for k in range(classes)]
    total = sums[0]
    for k in range(1, classes):
        total = total + sums[k]

    lane = lax.broadcasted_iota(jnp.int32, (here, 128), 1)
    fields = jnp.zeros((here, 128), F32)
    for n, v in enumerate((*sums, top, total, fixed, oid.astype(F32))):
        fields = jnp.where(lane == n, v, fields)
    fields = jnp.concatenate([fields, jnp.zeros((128 - here, 128), F32)], axis=0).T
    stat[...] = fields[0 : 2 * classes]
    pair = send(stat, pair_in, one_s.at[1], one_r.at[1], {"cls": other})
    pair.start()
    pair.wait()
    mine, theirs = stat[...], pair_in[...]
    top_a, top_b = mine[classes : classes + 1], theirs[classes : classes + 1]
    both = jnp.maximum(top_a, top_b)
    scale = jnp.exp(top_a - both)
    total = mine[classes + 1 : classes + 2] * scale + theirs[classes + 1 : classes + 2] * jnp.exp(top_b - both)
    prob = mine[0:classes] * scale / total
    prob_out[...] = prob[:, 0:here]
    weight = (mine[classes + 2 : classes + 3] * prob).astype(BF16).astype(F32)
    tile = jnp.concatenate([weight, mine[2 * classes - 1 :], jnp.zeros((classes - 1, 128), F32)], axis=0)
    tile = jnp.where(lax.broadcasted_iota(jnp.int32, tile.shape, 1) < here, tile, 0.0)
    packs = 128 // here
    mix[...] = pltpu.roll(tile, me_d % packs * here, 1)

    def mix_copy(i):
        return send(mix, mix_in.at[me_d], mix_s.at[i], mix_r.at[i], {"dom": (me_d + i) % doms})

    @pl.loop(1, doms)
    def _(i):
        mix_copy(i).start()

    mix_in[me_d] = mix[...]

    @pl.loop(1, half)
    def _(i):
        row_copy(i).wait()

    @pl.loop(half, doms)
    def _(i):
        part_copy(i, 0).wait()
        part_copy(i, 1).wait()

    @pl.loop(1, doms)
    def _(i):
        mix_copy(i).wait()

    got_mix = [jnp.sum(mix_in[n : n + packs], axis=0) for n in range(0, doms, packs)]
    got_mix = jnp.concatenate(got_mix, axis=1)
    wide = 2 * classes
    of_entry = jnp.broadcast_to(got_mix[classes : classes + 1].astype(jnp.int32), (wide, doms * here))
    weight = got_mix[0:classes]
    none = jnp.zeros_like(weight)

    def grow(part):
        rows = jnp.concatenate([weight, none] if part == 0 else [none, weight], axis=0)
        mixing = jnp.concatenate([jnp.where(of_entry == o, rows, 0.0) for o in range(zs)], axis=0)
        return jnp.dot(
            mixing.astype(BF16), in_rows[part].reshape(doms * here, band), preferred_element_type=F32
        )

    volume = grow(0) + grow(1)
    for o in range(zs):
        slab[o] = volume[o * wide : (o + 1) * wide].astype(BF16)

    def z_copy(i):
        return send(slab.at[(me_z + i) % zs], slab_in.at[i], z_s.at[i], z_r.at[i], {"orient": (me_z + i) % zs})

    for i in sorted(range(1, zs), key=lambda i: -min(i, zs - i)):
        z_copy(i).start()

    slab_in[0] = slab[me_z]

    @pl.loop(1, half)
    def _(j):
        plane_copy(j).wait_send()

    @pl.loop(0, steps * half)
    def _(n):
        s, j = 1 + n // half, n % half

        @pl.when((s < steps) | (j < half // 2))
        def _():
            ring_copy(0, s, j).wait_send()

        @pl.when((s < steps) | (j >= half // 2))
        def _():
            ring_copy(1, s, j).wait_send()

    @pl.loop(1, zs)
    def _(i):
        z_copy(i).wait()

    out = slab_in[0].astype(F32)
    for i in range(1, zs):
        out = out + slab_in[i].astype(F32)
    vol_out[...] = out


def tables():
    kx = np.arange(IMG) - IMG // 2
    ky = np.arange(IMG // 2)
    turn_x = 2 * np.pi / IMG * ((np.arange(TX) - TX // 2)[:, None] * kx[None, :])
    turn_y = 2 * np.pi / IMG * (ky[:, None] * (np.arange(TY) - TY // 2)[None, :])
    return [
        np.stack([np.cos(t), np.sin(t)]).astype(np.float32) for t in (turn_x, turn_y.reshape(-1))
    ]


def solution(mesh):
    doms, zs = mesh.shape["dom"], mesh.shape["orient"]

    def local(references, images, orient_lists, shift_ids, fixed_weights):
        classes, here = references.shape[1], images.shape[1]
        columns = classes * references.shape[2]
        band = images.shape[2] // doms
        half = doms // 2
        vmem, hbm = pl.BlockSpec(memory_space=pltpu.VMEM), pl.BlockSpec(memory_space=pltpu.MemorySpace.HBM)
        dma = pltpu.SemaphoreType.DMA
        rows = TX * here
        prob, volume = pl.pallas_call(
            functools.partial(kernel, doms, zs),
            out_shape=(
                jax.ShapeDtypeStruct((classes, here), F32),
                jax.ShapeDtypeStruct((2 * classes, band), F32),
            ),
            in_specs=[hbm] * 7,
            out_specs=(vmem, vmem),
            scratch_shapes=[
                pltpu.VMEM((2, here, images.shape[2]), BF16),
                pltpu.VMEM((2, TX, IMG), F32),
                pltpu.SMEM((2, IMG // 2 * TY), F32),
                pltpu.VMEM((1, here), jnp.int32),
                pltpu.VMEM((1, here), jnp.int32),
                pltpu.VMEM((1, here), F32),
                pltpu.VMEM((zs, half, 2, columns, IMG), BF16),
                pltpu.VMEM((half, 2, here, band), BF16),
                pltpu.VMEM((doms, 2, here, band), BF16),
                pltpu.VMEM((2, doms, here, band), BF16),
                pltpu.VMEM((2 * rows, 2 * IMG), BF16),
                pltpu.VMEM((TY * columns, 2 * IMG), BF16),
                pltpu.VMEM((2 * rows, 2 * IMG), BF16),
                pltpu.VMEM((TY * columns, 2 * IMG), BF16),
                pltpu.VMEM((2 * rows, TY * columns), F32),
                pltpu.VMEM((rows, TY * columns), F32),
                pltpu.VMEM((2 * classes, 128), F32),
                pltpu.VMEM((2 * classes, 128), F32),
                pltpu.VMEM((2 * classes, 128), F32),
                pltpu.VMEM((doms, 2 * classes, 128), F32),
                pltpu.VMEM((zs, 2 * classes, band), BF16),
                pltpu.VMEM((zs, 2 * classes, band), BF16),
                dma((half,)), dma((half,)),
                dma((half,)), dma((half,)),
                dma((doms + half,)), dma((doms + half,)),
                dma((2, zs // 2, half)), dma((2, zs // 2, half)),
                dma((2,)), dma((2,)),
                dma((doms,)), dma((doms,)),
                dma((zs,)), dma((zs,)),
                dma((7,)),
            ],
            compiler_params=pltpu.CompilerParams(
                collective_id=0, has_side_effects=True, vmem_limit_bytes=48 << 20
            ),
            name="estep",
        )(
            *[
                pltpu.with_memory_space_constraint(v, pltpu.MemorySpace.HBM)
                for v in (
                    references.reshape(2, columns, references.shape[3]),
                    images,
                    *[jnp.asarray(t) for t in tables()],
                    orient_lists.reshape(1, here),
                    shift_ids.reshape(1, here),
                    fixed_weights.reshape(1, here),
                )
            ]
        )
        return prob.T, volume.reshape(2, classes, 1, band)

    in_specs = (
        P(None, "cls", None, ("dom", "orient")),
        P(None, ("dom", "orient"), None),
        P(("dom", "orient"), None),
        P(("dom", "orient"), None),
        P(("dom", "orient"), None),
    )
    out_specs = (P(("dom", "orient"), "cls"), P(None, "cls", "orient", "dom"))
    return jax.shard_map(local, mesh=mesh, in_specs=in_specs, out_specs=out_specs, check_vma=False)
```

time: 79.8 us -> 61.5 us (0.77)
  Pallas kernels: 70.1 us -> 59.5 us
  local copies, waits for them, and re-layouts: 8.67 us -> 1.29 us
    pallas_call x1, Pallas kernels: 70.1 us -> 59.5 us  [local(): pl.pallas_call(functools.partial(kernel, doms, zs), out_shape=(jax.ShapeD...]
    unnamed x16 -> x1, local copies, waits for them, and re-layouts: 7.96 us -> 0.58 us
where the time goes in v3:
time: 61.5 us; the launch traced here: 61.4 us
  Pallas kernels  59.5 us (97%)
  local copies, waits for them, and re-layouts  1.29 us (2%)
  between operations  0.64 us (1%)
    pallas_call x1, Pallas kernels, local(): pl.pallas_call(functools.partial(kernel, doms, zs), out_shape=(jax.ShapeD...  59.5 us

profile of v3, /device:TPU:1, one launch (start us, length us, event | category | flops | bytes accessed | tf_op | source)
XLA Modules:
  0.0 61.4 jit_solution(1984041060213454538)
XLA Ops:
  0.6 59.5 %estep.1 = (f32[4,16]{1,0:T(4,128)S(1)}, f32[8,2048]{1,0:T(8,128)S(1)}) custom-call(bf16[2,32,256]{2,1,0:T(8,128)(2,1)} %bitcast.6, bf16[2,16,32768]{2,1,0:T(8,128)(2,1)} %images.1, f32[2,8,256]{2,1,0:T(8,128)} %constant.4.clone.xtab_in, f32[2,1024]{1,0:T(2,128)} %constant.5.clone.ytab_in, s32[1,16]{1,0:T(1,128)} %bitcast.7, s32[1,16]{1,0:T(1,128)} %bitcast.8, ...), custom_call_target="tpu_custom_call" | custom-call | tf_op jit(solution)/shard_map/estep/pallas_call | solution.py:420
  60.1 0.7 %reshape.24 = f32[2,4,1,2048]{3,2,1,0:T(1,128)} reshape(f32[8,2048]{1,0:T(8,128)S(1)} %get-tuple-element.5) | data formatting | bytes 131072 | tf_op jit(solution)/shard_map/reshape | solution.py:477
  60.8 0.6 copy.11

commit v4 on v3

--- a/solution.py
+++ b/solution.py
@@ -13,6 +13,7 @@
 TX = 8
 TY = 8
 MESH = pl.DeviceIdType.MESH
+NEAR_ROWS = 12
 F32 = jnp.float32
 BF16 = jnp.bfloat16
 
@@ -20,7 +21,7 @@
 def kernel(
     doms, zs, refs, images, xtab_in, ytab_in, oid_in, sid_in, fixed_in, prob_out, vol_out,
     imgs, xtab, ytab, oid_row, sid_row, fixed_row,
-    ref_all, sib, out_rows, in_rows, xs_a, rs_a, xs_b, rs_b, acc, got, stat, pair_in, mix, mix_in, slab, slab_in,
+    ref_all, sib, out_rows, in_rows, xs_a, rs_a, xs_b, rs_b, acc, got, stat, stat_in, slab, slab_in,
     plane_s, plane_r, sib_s, sib_r, row_s, row_r, ring_s, ring_r, one_s, one_r, mix_s, mix_r, z_s, z_r, in_s,
 ):
     here = images.shape[1]
@@ -32,10 +33,13 @@
     classes = columns // zs
     steps = zs // 2
     me_d, me_z, me_c = lax.axis_index("dom"), lax.axis_index("orient"), lax.axis_index("cls")
-    core, me_q = me_d % 2, me_d // 2
-    me_x, me_l = me_q % side, me_q // side
-    me_y = 2 * me_c + me_l
+    core, me_q = lax.rem(me_d, 2), lax.div(me_d, 2)
+    me_x, me_l = lax.rem(me_q, side), lax.div(me_q, side)
     twin = me_d + 1 - 2 * core
+
+    def wrap(v, n):
+        return jnp.where(v >= n, v - n, v)
+
     other = 1 - me_c
 
     def send(src, dst, s, r, to):
@@ -50,17 +54,15 @@
 
     @pl.loop(1, doms)
     def _(i):
-        greet({"dom": (me_d + i) % doms})
+        greet({"dom": wrap(me_d + i, doms)})
 
     @pl.loop(1, zs)
     def _(i):
-        greet({"orient": (me_z + i) % zs})
-
-    greet({"cls": other})
-
-    @pl.loop(0, half)
-    def _(i):
-        greet({"dom": half * (1 - me_l) + i, "cls": other})
+        greet({"orient": wrap(me_z + i, zs)})
+
+    @pl.loop(0, doms)
+    def _(i):
+        greet({"dom": i, "cls": other})
 
     loads = [
         pltpu.make_async_copy(src, dst, in_s.at[n])
@@ -78,24 +80,26 @@
     ]
     for load in loads:
         load.start()
-    pl.semaphore_wait(barrier, doms + zs - 1 + half)
+    pl.semaphore_wait(barrier, 2 * doms + zs - 2)
 
     def plane_copy(j):
-        to = (me_l + j // side) % 2 * side + (me_x + j % side) % side
+        low = wrap(j, side)
+        to = jnp.where(j < side, me_l, 1 - me_l) * side + wrap(me_x + low, side)
         at = ref_all.at[me_z, me_q]
         return send(at, at, plane_s.at[j], plane_r.at[j], {"dom": 2 * to + core})
 
     def piece(j):
-        return (me_l + j // side) % 2 * side + (me_x + side - j % side) % side
+        low = wrap(j, side)
+        return jnp.where(j < side, me_l, 1 - me_l) * side + wrap(me_x + side - low, side)
 
     def sib_copy(q):
         start = pl.multiple_of((2 * q + 1 - core) * band, band)
         return send(images.at[:, :, pl.ds(start, band)], sib.at[q], sib_s.at[q], sib_r.at[q], {"dom": twin})
 
-    right, left = (me_z + 1) % zs, (me_z + zs - 1) % zs
+    right, left = wrap(me_z + 1, zs), wrap(me_z + zs - 1, zs)
 
     def ring_copy(way, s, j):
-        block = (me_z + zs + 1 - s) % zs if way == 0 else (me_z + s - 1) % zs
+        block = wrap(me_z + zs + 1 - s, zs) if way == 0 else wrap(me_z + s - 1, zs)
         at = ref_all.at[block, piece(j)]
         return send(
             at, at, ring_s.at[way, s - 1, j], ring_r.at[way, s - 1, j], {"orient": right if way == 0 else left}
@@ -131,54 +135,53 @@
     at_x, at_y = shift & (TX - 1), shift >> 3
     twice = lambda v: jnp.concatenate([v, v], axis=1)
     wide_x = twice(at_x)
-    px_c = jnp.zeros((here, IMG), F32)
-    px_s = jnp.zeros((here, IMG), F32)
-    for a in range(TX):
-        px_c = jnp.where(wide_x == a, xcos[a : a + 1, :], px_c)
-        px_s = jnp.where(wide_x == a, xsin[a : a + 1, :], px_s)
+
+    def chosen(at, table, shape):
+        out = jnp.zeros(shape, F32)
+        for n in range(TX):
+            out = jnp.where(at == n, table(n), out)
+        return out
+
+    def phase_y(line):
+        c = chosen(at_y, lambda n: ycos(line * TY + n), (here, 128))
+        s = chosen(at_y, lambda n: ysin(line * TY + n), (here, 128))
+        return twice(c), twice(s)
+
+    px_c = chosen(wide_x, lambda n: xcos[n : n + 1, :], (here, IMG))
+    px_s = chosen(wide_x, lambda n: xsin[n : n + 1, :], (here, IMG))
+    turn_c, turn_s = phase_y(1)
+
+    def turned(line):
+        c, s = phase_y(line)
+        return px_c * c - px_s * s, px_s * c + px_c * s
 
     def band_of(i):
-        return 2 * ((me_l + i // half) % 2 * side + (me_x + i // 2 % side) % side) + (core + i % 2) % 2
+        low = wrap(i, half)
+        hop = lax.div(low, 2)
+        flip = low - 2 * hop
+        to = jnp.where(i < half, me_l, 1 - me_l) * side + wrap(me_x + hop, side)
+        return 2 * to + jnp.where(flip == 0, core, 1 - core)
 
     def row_copy(i):
-        return send(out_rows.at[i], in_rows.at[:, me_d], row_s.at[i], row_r.at[i], {"dom": band_of(i)})
-
-    def part_copy(i, r):
-        n = i + r * half
-        y = (me_y + (1 if r == 0 else 3)) % 4
-        return send(
-            out_rows.at[i, r], in_rows.at[r, me_d], row_s.at[n], row_r.at[n], {"dom": band_of(i), "cls": y // 2}
-        )
+        to = {"dom": band_of(i), "cls": jnp.where(i < NEAR_ROWS, me_c, other)}
+        return send(out_rows.at[i], in_rows.at[:, me_d], row_s.at[i], row_r.at[i], to)
 
     @pl.loop(0, doms)
     def _(i):
         d = band_of(i)
 
-        @pl.loop(0, lines)
-        def _(r):
-            col = pl.multiple_of(d * band + r * IMG, IMG)
-            re = imgs[0, :, pl.ds(col, IMG)].astype(F32)
-            im = imgs[1, :, pl.ds(col, IMG)].astype(F32)
-            py_c = jnp.zeros((here, 128), F32)
-            py_s = jnp.zeros((here, 128), F32)
-            for b in range(TY):
-                py_c = jnp.where(at_y == b, ycos((d * lines + r) * TY + b), py_c)
-                py_s = jnp.where(at_y == b, ysin((d * lines + r) * TY + b), py_s)
-            py_c, py_s = twice(py_c), twice(py_s)
-            c = px_c * py_c - px_s * py_s
-            s = px_s * py_c + px_c * py_s
-            to = pl.ds(pl.multiple_of(r * IMG, IMG), IMG)
-            out_rows[i, 0, :, to] = (re * c - im * s).astype(BF16)
-            out_rows[i, 1, :, to] = (re * s + im * c).astype(BF16)
-
-        @pl.when((i > 0) & (i < half))
+        c, s = turned(d * lines)
+        for r in range(lines):
+            if r > 0:
+                c, s = c * turn_c - s * turn_s, c * turn_s + s * turn_c
+            col = pl.ds(pl.multiple_of(d * band + r * IMG, IMG), IMG)
+            re, im = imgs[0, :, col].astype(F32), imgs[1, :, col].astype(F32)
+            out_rows[i, 0, :, r * IMG : (r + 1) * IMG] = (re * c - im * s).astype(BF16)
+            out_rows[i, 1, :, r * IMG : (r + 1) * IMG] = (re * s + im * c).astype(BF16)
+
+        @pl.when(i > 0)
         def _():
             row_copy(i).start()
-
-        @pl.when(i >= half)
-        def _():
-            part_copy(i, 0).start()
-            part_copy(i, 1).start()
 
     in_rows[:, me_d] = out_rows[0]
 
@@ -234,28 +237,35 @@
             xs[...], rs[...], (((1,), (1,)), ((), ())), preferred_element_type=F32
         )
 
-    @pl.loop(0, half)
-    def _(q):
-        sib_copy(q).wait()
-
     first, middle = half // 2, half * (steps - 1)
 
     @pl.loop(0, half + middle)
     def _(t):
-        @pl.when(t < first)
-        def _():
-            for n in range(2):
-                j = 2 * t + n
-
-                @pl.when(j > 0)
+        u = t - first
+        s = 1
+        for k in range(1, steps - 1):
+            s = jnp.where(u >= k * half, k + 1, s)
+        j = u - half * (s - 1)
+        m = t - first - middle
+        at_first, at_last = t < first, m >= 0
+        j_a = jnp.where(at_last, m, jnp.where(at_first, 2 * t, j))
+        j_b = jnp.where(at_last, m + half // 2, jnp.where(at_first, 2 * t + 1, j))
+
+        @pl.when(at_first)
+        def _():
+            for c in (j_a, j_b):
+
+                @pl.when(c > 0)
                 def _():
-                    plane_copy(j).wait_recv()
-                    ring_copy(0, 1, j).start()
-                    ring_copy(1, 1, j).start()
-
-        @pl.when((t >= first) & (t < first + middle))
-        def _():
-            s, j = 1 + (t - first) // half, (t - first) % half
+                    plane_copy(c).wait_recv()
+                    ring_copy(0, 1, c).start()
+                    ring_copy(1, 1, c).start()
+
+            for c in (j_a, j_b):
+                sib_copy(piece(c)).wait()
+
+        @pl.when((t >= first) & (m < 0))
+        def _():
             ring_copy(0, s, j).wait_recv()
 
             @pl.when((s < steps - 1) | (j < half // 2))
@@ -268,20 +278,15 @@
             def _():
                 ring_copy(1, s + 1, j).start()
 
-        @pl.when(t >= first + middle)
-        def _():
-            j = t - first - middle
-            ring_copy(0, steps, j).wait_recv()
-            ring_copy(1, steps, j + half // 2).wait_recv()
-
-        at_first, at_last = t < first, t >= first + middle
-        s, j = 1 + (t - first) // half, (t - first) % half
+        @pl.when(at_last)
+        def _():
+            ring_copy(0, steps, j_a).wait_recv()
+            ring_copy(1, steps, j_b).wait_recv()
+
         near = jnp.where(at_last, steps, jnp.where(at_first, 0, s))
-        j_a = jnp.where(at_last, t - first - middle, jnp.where(at_first, 2 * t, j))
-        j_b = jnp.where(at_last, j_a + half // 2, jnp.where(at_first, 2 * t + 1, j))
-        prepare(xs_a, rs_a, (me_z + zs - near) % zs, piece(j_a))
+        prepare(xs_a, rs_a, wrap(me_z + zs - near, zs), piece(j_a))
         add(xs_b, rs_b)
-        prepare(xs_b, rs_b, (me_z + near) % zs, piece(j_b))
+        prepare(xs_b, rs_b, wrap(me_z + near, zs), piece(j_b))
         add(xs_a, rs_a)
 
     add(xs_b, rs_b)
@@ -305,50 +310,51 @@
     for n, v in enumerate((*sums, top, total, fixed, oid.astype(F32))):
         fields = jnp.where(lane == n, v, fields)
     fields = jnp.concatenate([fields, jnp.zeros((128 - here, 128), F32)], axis=0).T
-    stat[...] = fields[0 : 2 * classes]
-    pair = send(stat, pair_in, one_s.at[1], one_r.at[1], {"cls": other})
-    pair.start()
-    pair.wait()
-    mine, theirs = stat[...], pair_in[...]
-    top_a, top_b = mine[classes : classes + 1], theirs[classes : classes + 1]
-    both = jnp.maximum(top_a, top_b)
-    scale = jnp.exp(top_a - both)
-    total = mine[classes + 1 : classes + 2] * scale + theirs[classes + 1 : classes + 2] * jnp.exp(top_b - both)
-    prob = mine[0:classes] * scale / total
-    prob_out[...] = prob[:, 0:here]
-    weight = (mine[classes + 2 : classes + 3] * prob).astype(BF16).astype(F32)
-    tile = jnp.concatenate([weight, mine[2 * classes - 1 :], jnp.zeros((classes - 1, 128), F32)], axis=0)
-    tile = jnp.where(lax.broadcasted_iota(jnp.int32, tile.shape, 1) < here, tile, 0.0)
     packs = 128 // here
-    mix[...] = pltpu.roll(tile, me_d % packs * here, 1)
-
-    def mix_copy(i):
-        return send(mix, mix_in.at[me_d], mix_s.at[i], mix_r.at[i], {"dom": (me_d + i) % doms})
+    mark = lax.rem(me_d, packs) * here
+    stat[...] = pltpu.roll(fields[0 : 2 * classes], mark, 1)
+
+    def stat_copy(far, i):
+        to = {"dom": wrap(me_d + i, doms), "cls": other} if far else {"dom": wrap(me_d + i, doms)}
+        return send(stat, stat_in.at[me_c, me_d], mix_s.at[far, i], mix_r.at[far, i], to)
+
+    @pl.loop(0, doms)
+    def _(i):
+        stat_copy(1, i).start()
+
+        @pl.when(i > 0)
+        def _():
+            stat_copy(0, i).start()
+
+    stat_in[me_c, me_d] = stat[...]
 
     @pl.loop(1, doms)
     def _(i):
-        mix_copy(i).start()
-
-    mix_in[me_d] = mix[...]
-
-    @pl.loop(1, half)
-    def _(i):
         row_copy(i).wait()
 
-    @pl.loop(half, doms)
-    def _(i):
-        part_copy(i, 0).wait()
-        part_copy(i, 1).wait()
-
-    @pl.loop(1, doms)
-    def _(i):
-        mix_copy(i).wait()
-
-    got_mix = [jnp.sum(mix_in[n : n + packs], axis=0) for n in range(0, doms, packs)]
-    got_mix = jnp.concatenate(got_mix, axis=1)
+    @pl.loop(0, doms)
+    def _(i):
+        stat_copy(1, i).wait()
+
+        @pl.when(i > 0)
+        def _():
+            stat_copy(0, i).wait()
+
+    def shares(mine, theirs):
+        top_a, top_b = mine[classes : classes + 1], theirs[classes : classes + 1]
+        both = jnp.maximum(top_a, top_b)
+        scale = jnp.exp(top_a - both)
+        total = mine[classes + 1 : classes + 2] * scale + theirs[classes + 1 : classes + 2] * jnp.exp(top_b - both)
+        return mine[0:classes] * scale / total
+
+    def joined(c):
+        sums = [jnp.sum(stat_in[c, n : n + packs], axis=0) for n in range(0, doms, packs)]
+        return jnp.concatenate(sums, axis=1)
+
+    mine = joined(me_c)
+    weight = (mine[classes + 2 : classes + 3] * shares(mine, joined(other))).astype(BF16).astype(F32)
     wide = 2 * classes
-    of_entry = jnp.broadcast_to(got_mix[classes : classes + 1].astype(jnp.int32), (wide, doms * here))
-    weight = got_mix[0:classes]
+    of_entry = jnp.broadcast_to(mine[2 * classes - 1 :].astype(jnp.int32), (wide, doms * here))
     none = jnp.zeros_like(weight)
 
     def grow(part):
@@ -363,12 +369,17 @@
         slab[o] = volume[o * wide : (o + 1) * wide].astype(BF16)
 
     def z_copy(i):
-        return send(slab.at[(me_z + i) % zs], slab_in.at[i], z_s.at[i], z_r.at[i], {"orient": (me_z + i) % zs})
+        return send(slab.at[wrap(me_z + i, zs)], slab_in.at[i], z_s.at[i], z_r.at[i], {"orient": wrap(me_z + i, zs)})
 
     for i in sorted(range(1, zs), key=lambda i: -min(i, zs - i)):
         z_copy(i).start()
 
     slab_in[0] = slab[me_z]
+    live = lax.broadcasted_iota(jnp.int32, stat.shape, 1) - mark
+    live = (live >= 0) & (live < here)
+    prob = shares(jnp.where(live, stat[...], 1.0), jnp.where(live, stat_in[other, me_d], 1.0))
+    prob = pltpu.roll(jnp.concatenate([prob, prob], axis=0), 128 - mark, 1)
+    prob_out[...] = prob[0:classes, 0:here]
 
     @pl.loop(1, half)
     def _(j):
@@ -376,7 +387,8 @@
 
     @pl.loop(0, steps * half)
     def _(n):
-        s, j = 1 + n // half, n % half
+        s = 1 + lax.div(n, half)
+        j = n - half * (s - 1)
 
         @pl.when((s < steps) | (j < half // 2))
         def _():
@@ -443,17 +455,15 @@
                 pltpu.VMEM((2 * rows, TY * columns), F32),
                 pltpu.VMEM((rows, TY * columns), F32),
                 pltpu.VMEM((2 * classes, 128), F32),
-                pltpu.VMEM((2 * classes, 128), F32),
-                pltpu.VMEM((2 * classes, 128), F32),
-                pltpu.VMEM((doms, 2 * classes, 128), F32),
+                pltpu.VMEM((2, doms, 2 * classes, 128), F32),
                 pltpu.VMEM((zs, 2 * classes, band), BF16),
                 pltpu.VMEM((zs, 2 * classes, band), BF16),
                 dma((half,)), dma((half,)),
                 dma((half,)), dma((half,)),
-                dma((doms + half,)), dma((doms + half,)),
+                dma((doms,)), dma((doms,)),
                 dma((2, zs // 2, half)), dma((2, zs // 2, half)),
-                dma((2,)), dma((2,)),
-                dma((doms,)), dma((doms,)),
+                dma((1,)), dma((1,)),
+                dma((2, doms)), dma((2, doms)),
                 dma((zs,)), dma((zs,)),
                 dma((7,)),
             ],

time: 61.5 us -> 58.6 us (0.953)
  Pallas kernels: 59.5 us -> 56.5 us
    pallas_call x1, Pallas kernels: 59.5 us -> 56.5 us  [local(): pl.pallas_call(functools.partial(kernel, doms, zs), out_shape=(jax.ShapeD...]
where the time goes in v4:
time: 58.6 us; the launch traced here: 58.5 us
  Pallas kernels  56.5 us (96%)
  local copies, waits for them, and re-layouts  1.29 us (2%)
  between operations  0.64 us (1%)
    pallas_call x1, Pallas kernels, local(): pl.pallas_call(functools.partial(kernel, doms, zs), out_shape=(jax.ShapeD...  56.5 us

profile of v4, /device:TPU:1, one launch (start us, length us, event | category | flops | bytes accessed | tf_op | source)
XLA Modules:
  0.0 58.5 jit_solution(4578889490389951363)
XLA Ops:
  0.6 56.5 %estep.1 = (f32[4,16]{1,0:T(4,128)S(1)}, f32[8,2048]{1,0:T(8,128)S(1)}) custom-call(bf16[2,32,256]{2,1,0:T(8,128)(2,1)} %bitcast.6, bf16[2,16,32768]{2,1,0:T(8,128)(2,1)} %images.1, f32[2,8,256]{2,1,0:T(8,128)} %constant.4.clone.xtab_in, f32[2,1024]{1,0:T(2,128)} %constant.5.clone.ytab_in, s32[1,16]{1,0:T(1,128)} %bitcast.7, s32[1,16]{1,0:T(1,128)} %bitcast.8, ...), custom_call_target="tpu_custom_call" | custom-call | tf_op jit(solution)/shard_map/estep/pallas_call | solution.py:432
  57.2 0.7 %reshape.24 = f32[2,4,1,2048]{3,2,1,0:T(1,128)} reshape(f32[8,2048]{1,0:T(8,128)S(1)} %get-tuple-element.5) | data formatting | bytes 131072 | tf_op jit(solution)/shard_map/reshape | solution.py:487
  57.9 0.6 copy.11

commit v5 on v4

--- a/solution.py
+++ b/solution.py
@@ -13,7 +13,6 @@
 TX = 8
 TY = 8
 MESH = pl.DeviceIdType.MESH
-NEAR_ROWS = 12
 F32 = jnp.float32
 BF16 = jnp.bfloat16
 
@@ -163,8 +162,16 @@
         return 2 * to + jnp.where(flip == 0, core, 1 - core)
 
     def row_copy(i):
-        to = {"dom": band_of(i), "cls": jnp.where(i < NEAR_ROWS, me_c, other)}
-        return send(out_rows.at[i], in_rows.at[:, me_d], row_s.at[i], row_r.at[i], to)
+        return send(out_rows.at[i], in_rows.at[:, me_d], row_s.at[i], row_r.at[i], {"dom": band_of(i)})
+
+    me_y = 2 * me_c + me_l
+    cls_of = [lax.div(wrap(me_y + 1, 4), 2), lax.div(wrap(me_y + 3, 4), 2)]
+
+    def part_copy(i, r):
+        n = i + r * half
+        return send(
+            out_rows.at[i, r], in_rows.at[r, me_d], row_s.at[n], row_r.at[n], {"dom": band_of(i), "cls": cls_of[r]}
+        )
 
     @pl.loop(0, doms)
     def _(i):
@@ -179,9 +186,14 @@
             out_rows[i, 0, :, r * IMG : (r + 1) * IMG] = (re * c - im * s).astype(BF16)
             out_rows[i, 1, :, r * IMG : (r + 1) * IMG] = (re * s + im * c).astype(BF16)
 
-        @pl.when(i > 0)
+        @pl.when((i > 0) & (i < half))
         def _():
             row_copy(i).start()
+
+        @pl.when(i >= half)
+        def _():
+            part_copy(i, 0).start()
+            part_copy(i, 1).start()
 
     in_rows[:, me_d] = out_rows[0]
 
@@ -310,9 +322,8 @@
     for n, v in enumerate((*sums, top, total, fixed, oid.astype(F32))):
         fields = jnp.where(lane == n, v, fields)
     fields = jnp.concatenate([fields, jnp.zeros((128 - here, 128), F32)], axis=0).T
-    packs = 128 // here
-    mark = lax.rem(me_d, packs) * here
-    stat[...] = pltpu.roll(fields[0 : 2 * classes], mark, 1)
+    kinds = 2 * classes
+    stat[...] = jnp.sum(pltpu.roll(fields[0:kinds], 0, 1, stride=here, stride_axis=0), axis=0, keepdims=True)
 
     def stat_copy(far, i):
         to = {"dom": wrap(me_d + i, doms), "cls": other} if far else {"dom": wrap(me_d + i, doms)}
@@ -328,10 +339,15 @@
 
     stat_in[me_c, me_d] = stat[...]
 
-    @pl.loop(1, doms)
+    @pl.loop(1, half)
     def _(i):
         row_copy(i).wait()
 
+    @pl.loop(half, doms)
+    def _(i):
+        part_copy(i, 0).wait()
+        part_copy(i, 1).wait()
+
     @pl.loop(0, doms)
     def _(i):
         stat_copy(1, i).wait()
@@ -340,21 +356,34 @@
         def _():
             stat_copy(0, i).wait()
 
-    def shares(mine, theirs):
-        top_a, top_b = mine[classes : classes + 1], theirs[classes : classes + 1]
+    packs = 128 // here
+    of_sender = lax.broadcasted_iota(jnp.int32, (packs, 128), 1) // here == lax.broadcasted_iota(
+        jnp.int32, (packs, 128), 0
+    )
+
+    def unpacked(c, names):
+        tiles = [stat_in[c, n : n + packs].reshape(packs, 128) for n in range(0, doms, packs)]
+
+        def field(f):
+            turned = [pltpu.roll(v, (128 - f * here) % 128, 1) for v in tiles]
+            turned = [pltpu.roll(v, 0, 1, stride=here, stride_axis=0) for v in turned]
+            return jnp.concatenate(
+                [jnp.sum(jnp.where(of_sender, v, 0.0), axis=0, keepdims=True) for v in turned], axis=1
+            )
+
+        return [field(f) for f in names]
+
+    def norm(top_a, total_a, top_b, total_b):
         both = jnp.maximum(top_a, top_b)
         scale = jnp.exp(top_a - both)
-        total = mine[classes + 1 : classes + 2] * scale + theirs[classes + 1 : classes + 2] * jnp.exp(top_b - both)
-        return mine[0:classes] * scale / total
-
-    def joined(c):
-        sums = [jnp.sum(stat_in[c, n : n + packs], axis=0) for n in range(0, doms, packs)]
-        return jnp.concatenate(sums, axis=1)
-
-    mine = joined(me_c)
-    weight = (mine[classes + 2 : classes + 3] * shares(mine, joined(other))).astype(BF16).astype(F32)
+        return scale, total_a * scale + total_b * jnp.exp(top_b - both)
+
+    *mine, top_a, total_a, fixed_a, oid_a = unpacked(me_c, range(kinds))
+    scale, total = norm(top_a, total_a, *unpacked(other, (classes, classes + 1)))
+    mine = jnp.concatenate(mine, axis=0)
+    weight = (fixed_a * (mine * scale / total)).astype(BF16).astype(F32)
     wide = 2 * classes
-    of_entry = jnp.broadcast_to(mine[2 * classes - 1 :].astype(jnp.int32), (wide, doms * here))
+    of_entry = jnp.broadcast_to(oid_a.astype(jnp.int32), (wide, doms * here))
     none = jnp.zeros_like(weight)
 
     def grow(part):
@@ -375,11 +404,11 @@
         z_copy(i).start()
 
     slab_in[0] = slab[me_z]
-    live = lax.broadcasted_iota(jnp.int32, stat.shape, 1) - mark
-    live = (live >= 0) & (live < here)
-    prob = shares(jnp.where(live, stat[...], 1.0), jnp.where(live, stat_in[other, me_d], 1.0))
-    prob = pltpu.roll(jnp.concatenate([prob, prob], axis=0), 128 - mark, 1)
-    prob_out[...] = prob[0:classes, 0:here]
+    own, far = stat[...], stat_in[other, me_d]
+    cut = lambda row, f: row[:, f * here : (f + 1) * here]
+    scale, total = norm(cut(own, classes), cut(own, classes + 1), cut(far, classes), cut(far, classes + 1))
+    for k in range(classes):
+        prob_out[k : k + 1, :] = cut(own, k) * scale / total
 
     @pl.loop(1, half)
     def _(j):
@@ -454,13 +483,13 @@
                 pltpu.VMEM((TY * columns, 2 * IMG), BF16),
                 pltpu.VMEM((2 * rows, TY * columns), F32),
                 pltpu.VMEM((rows, TY * columns), F32),
-                pltpu.VMEM((2 * classes, 128), F32),
-                pltpu.VMEM((2, doms, 2 * classes, 128), F32),
+                pltpu.VMEM((1, 128), F32),
+                pltpu.VMEM((2, doms, 1, 128), F32),
                 pltpu.VMEM((zs, 2 * classes, band), BF16),
                 pltpu.VMEM((zs, 2 * classes, band), BF16),
                 dma((half,)), dma((half,)),
                 dma((half,)), dma((half,)),
-                dma((doms,)), dma((doms,)),
+                dma((doms + half,)), dma((doms + half,)),
                 dma((2, zs // 2, half)), dma((2, zs // 2, half)),
                 dma((1,)), dma((1,)),
                 dma((2, doms)), dma((2, doms)),

time: 58.6 us -> 57.5 us (0.981)
  Pallas kernels: 56.5 us -> 55.4 us
    pallas_call x1, Pallas kernels: 56.5 us -> 55.4 us  [local(): pl.pallas_call(functools.partial(kernel, doms, zs), out_shape=(jax.ShapeD...]
where the time goes in v5:
time: 57.5 us; the launch traced here: 57.4 us
  Pallas kernels  55.4 us (96%)
  local copies, waits for them, and re-layouts  1.29 us (2%)
  between operations  0.64 us (1%)
    pallas_call x1, Pallas kernels, local(): pl.pallas_call(functools.partial(kernel, doms, zs), out_shape=(jax.ShapeD...  55.4 us

profile of v5, /device:TPU:1, one launch (start us, length us, event | category | flops | bytes accessed | tf_op | source)
XLA Modules:
  0.0 57.4 jit_solution(2974146845678994983)
XLA Ops:
  0.6 55.4 %estep.1 = (f32[4,16]{1,0:T(4,128)S(1)}, f32[8,2048]{1,0:T(8,128)S(1)}) custom-call(bf16[2,32,256]{2,1,0:T(8,128)(2,1)} %bitcast.6, bf16[2,16,32768]{2,1,0:T(8,128)(2,1)} %images.1, f32[2,8,256]{2,1,0:T(8,128)} %constant.4.clone.xtab_in, f32[2,1024]{1,0:T(2,128)} %constant.5.clone.ytab_in, s32[1,16]{1,0:T(1,128)} %bitcast.7, s32[1,16]{1,0:T(1,128)} %bitcast.8, ...), custom_call_target="tpu_custom_call" | custom-call | tf_op jit(solution)/shard_map/estep/pallas_call | solution.py:461
  56.1 0.7 %reshape.24 = f32[2,4,1,2048]{3,2,1,0:T(1,128)} reshape(f32[8,2048]{1,0:T(8,128)S(1)} %get-tuple-element.5) | data formatting | bytes 131072 | tf_op jit(solution)/shard_map/reshape | solution.py:516
  56.8 0.6 %copy.11 = f32[16,4]{0,1:T(4,128)} copy(f32[16,4]{0,1:T(4,128)S(1)} %bitcast.5) | data formatting | bytes 512

commit v6 on v5

--- a/solution.py
+++ b/solution.py
@@ -113,8 +113,8 @@
         plane_copy(j).start()
 
     @pl.loop(0, half)
-    def _(q):
-        sib_copy(q).start()
+    def _(j):
+        sib_copy(piece(j)).start()
 
     for load in loads[1:]:
         load.wait()

time: 57.5 us -> 57.4 us (level)
  no operation moved by 1% of the time
where the time goes in v6:
time: 57.4 us; the launch traced here: 57.3 us
  Pallas kernels  55.4 us (97%)
  local copies, waits for them, and re-layouts  1.29 us (2%)
  between operations  0.64 us (1%)
    pallas_call x1, Pallas kernels, local(): pl.pallas_call(functools.partial(kernel, doms, zs), out_shape=(jax.ShapeD...  55.4 us

profile of v6, /device:TPU:1, one launch (start us, length us, event | category | flops | bytes accessed | tf_op | source)
XLA Modules:
  0.0 57.3 jit_solution(12636609003203260798)
XLA Ops:
  0.6 55.4 %estep.1 = (f32[4,16]{1,0:T(4,128)S(1)}, f32[8,2048]{1,0:T(8,128)S(1)}) custom-call(bf16[2,32,256]{2,1,0:T(8,128)(2,1)} %bitcast.6, bf16[2,16,32768]{2,1,0:T(8,128)(2,1)} %images.1, f32[2,8,256]{2,1,0:T(8,128)} %constant.4.clone.xtab_in, f32[2,1024]{1,0:T(2,128)} %constant.5.clone.ytab_in, s32[1,16]{1,0:T(1,128)} %bitcast.7, s32[1,16]{1,0:T(1,128)} %bitcast.8, ...), custom_call_target="tpu_custom_call" | custom-call | tf_op jit(solution)/shard_map/estep/pallas_call | solution.py:461
  56.0 0.7 %reshape.24 = f32[2,4,1,2048]{3,2,1,0:T(1,128)} reshape(f32[8,2048]{1,0:T(8,128)S(1)} %get-tuple-element.5) | data formatting | bytes 131072 | tf_op jit(solution)/shard_map/reshape | solution.py:516
  56.7 0.6 %copy.11 = f32[16,4]{0,1:T(4,128)} copy(f32[16,4]{0,1:T(4,128)S(1)} %bitcast.5) | data formatting | bytes 512
